TPU v7x, 768 devices: a whole 4x8x12 slice. The times are simulated.
768 devices in a mesh: ctx: 96 (over z, x, core), head: 8 (over y).
Axes of the slice: x: 4, y: 8, z: 12, core: 2. Of those that a mesh axis runs over, the one named last changes fastest.
Arguments:
- queries: float32 [2, 12288, 2048], P(None, 'ctx', 'head'), may hold values from -6 to 6
- keys: float32 [12288, 2048], P('ctx', 'head'), may hold values from -6 to 6
- values: float32 [12288, 2048], P('ctx', 'head'), may hold values from -6 to 6
- rates: float32 [12288, 8], P('ctx', 'head'), may hold values from 0.02 to 0.2
- grad_out: float32 [2, 12288, 2048], P(None, 'ctx', 'head'), may hold values from -6 to 6
- w_gate: float32 [8, 256, 512], P('head'), may hold values from -0.375 to 0.375
- w_up: float32 [8, 256, 512], P('head'), may hold values from -0.375 to 0.375
- w_down: float32 [8, 512, 256], P('head'), may hold values from -0.25 to 0.25
Outputs:
- grad_queries: float32 [2, 12288, 2048], P(None, 'ctx', 'head')
- grad_keys: float32 [12288, 2048], P('ctx', 'head')
- grad_values: float32 [12288, 2048], P('ctx', 'head')
All inputs are finite; a program needn't handle non-finite values.
Results may differ from a plain program's by a relative error of at most 0.00013.
Values sent between devices are 32-bit elements; how exact they have to be, the bound alone decides.
No kernel may reach another device: no remote copies, remote signals or barrier semaphores. Data moves between devices by JAX's collectives and lax.ppermute only.
A program may use at most 32 MiB of HBM per device.

v0:
```python
import jax
import jax.numpy as jnp
from jax import lax
from jax.sharding import PartitionSpec as P


def apply_fast(weights, inputs):
    w_gate, w_up, w_down = weights
    best = lax.Precision.HIGHEST
    gate = jnp.dot(inputs, w_gate, precision=best)
    up_part = jnp.dot(inputs, w_up, precision=best)
    return jnp.dot(jax.nn.silu(gate) * up_part, w_down, precision=best)


def inner_score(weights, keys_head, values_head, rates_head):
    return jnp.sum(rates_head[:, None] * apply_fast(weights, keys_head) * values_head)


def query_grad(weights, rows, cot_rows):
    pull = jax.vjp(lambda y: apply_fast(weights, y), rows)[1]
    return pull(cot_rows)[0]


def forward_parts(weights, rows, cot_rows):
    w_gate, w_up, w_down = weights
    best = lax.Precision.HIGHEST
    gate = jnp.dot(rows, w_gate, precision=best)
    up_part = jnp.dot(rows, w_up, precision=best)
    sigma = jax.nn.sigmoid(gate)
    active = gate * sigma
    hidden = active * up_part
    down_grad = jnp.dot(hidden.T, cot_rows, precision=best)
    return (gate, up_part, sigma, active, down_grad)


def inner_parts(weights, rows, cot_rows, gate, up_part, sigma, active):
    w_gate, w_up, w_down = weights
    best = lax.Precision.HIGHEST
    hidden_grad = jnp.dot(cot_rows, w_down.T, precision=best)
    up_grad = hidden_grad * active
    gate_grad = hidden_grad * up_part * sigma * (1.0 + gate * (1.0 - sigma))
    wg_grad = jnp.dot(rows.T, gate_grad, precision=best)
    wu_grad = jnp.dot(rows.T, up_grad, precision=best)
    row_grad = jnp.dot(gate_grad, w_gate.T, precision=best) + jnp.dot(
        up_grad, w_up.T, precision=best
    )
    return (wg_grad, wu_grad, row_grad)


def body(queries, keys, values, rates, grad_out, w_gate, w_up, w_down):
    heads = w_gate.shape[0]
    width = w_gate.shape[1]
    tok = keys.shape[0]
    scale = float(tok * lax.axis_size("ctx")) ** (-0.5)
    per_query = queries.reshape(2, tok, heads, width).transpose(2, 0, 1, 3)
    per_cot = grad_out.reshape(2, tok, heads, width).transpose(2, 0, 1, 3)
    per_key = keys.reshape(tok, heads, width).transpose(1, 0, 2)
    per_value = values.reshape(tok, heads, width).transpose(1, 0, 2)
    per_rate = rates.T
    initial = (w_gate, w_up, w_down)
    inner = jax.vmap(jax.grad(inner_score))(initial, per_key, per_value, per_rate)
    totals = lax.psum((inner[0], inner[1], inner[2]), "ctx")
    updated = tuple((w + scale * g for w, g in zip(initial, totals)))
    query_one = per_query[:, 1]
    cot_one = per_cot[:, 1]
    gate, up_part, sigma, active, down_local = jax.vmap(forward_parts)(updated, query_one, cot_one)
    wg_local, wu_local, grad_one = jax.vmap(inner_parts)(
        updated, query_one, cot_one, gate, up_part, sigma, active
    )
    direction = lax.psum((wg_local, wu_local, down_local), "ctx")

    def coupled_grads(weights, dirs, key_rows, value_rows, rate_rows):

        def coupled(key_in, value_in):
            tangent = jax.jvp(
                lambda ww: inner_score(ww, key_in, value_in, rate_rows), (weights,), (dirs,)
            )[1]
            return scale * tangent

        return jax.grad(coupled, argnums=(0, 1))(key_rows, value_rows)

    grad_key, grad_value = jax.vmap(coupled_grads)(initial, direction, per_key, per_value, per_rate)
    grad_zero = jax.vmap(query_grad)(initial, per_query[:, 0], per_cot[:, 0])
    grad_queries = (
        jnp.stack([grad_zero, grad_one], axis=1)
        .transpose(1, 2, 0, 3)
        .reshape(2, tok, heads * width)
    )
    grad_keys = grad_key.transpose(1, 0, 2).reshape(tok, heads * width)
    grad_values = grad_value.transpose(1, 0, 2).reshape(tok, heads * width)
    return (grad_queries, grad_keys, grad_values)


def solution(mesh):
    in_specs = (
        P(None, "ctx", "head"),
        P("ctx", "head"),
        P("ctx", "head"),
        P("ctx", "head"),
        P(None, "ctx", "head"),
        P("head", None, None),
        P("head", None, None),
        P("head", None, None),
    )
    out_specs = (P(None, "ctx", "head"), P("ctx", "head"), P("ctx", "head"))
    return jax.shard_map(body, mesh=mesh, in_specs=in_specs, out_specs=out_specs, check_vma=False)
```

profile of v0, /device:TPU:1, one launch (start us, length us, event | category | flops | bytes accessed | tf_op | source)
XLA Modules:
  0.0 609.2 jit_solution(17352935528963691179)
XLA Ops:
  7.2 0.0 copy-start
  7.2 0.0 all-reduce.7.cloned.1.call-start
  7.2 0.8 copy-done
  8.1 1.5 fusion.25
  9.5 0.0 copy-done.1
  9.6 0.0 copy-start.2
  9.6 0.0 copy-start.8
  9.6 0.4 fusion.11
  10.0 0.0 copy-start.26
  10.0 0.6 copy-done.2
  10.6 0.0 copy-done.8
  10.6 0.1 copy-done.26
  10.7 0.7 fusion.20
  11.4 1.5 convolution_bitcast_fusion.4
  12.9 1.4 convolution_bitcast_fusion.2
  14.4 1.4 convolution_bitcast_fusion.3
  15.8 0.0 all-reduce.7.cloned.1.call-update
  15.8 0.0 copy-start.3
  15.8 0.2 all-reduce.5.cloned.1.call-start
  16.1 0.7 copy-done.23
  16.7 0.6 fusion.22
  17.4 0.2 copy.15
  17.6 1.0 copy.11
  18.6 0.2 copy.13
  18.8 0.7 copy-done.13
  19.6 0.4 fusion.28
  20.0 1.1 convolution_multiply_fusion
  21.2 1.3 fusion.14
  22.5 282.5 %all-reduce.7.cloned.1.call-done = (f32[1,256,512]{1,2,0:T(8,128)}, f32[1,512,256]{1,2,0:T(8,128)}, f32[1,256,512]{1,2,0:T(8,128)}) async-done(((f32[1,256,512]{1,2,0:T(8,128)}, f32[1,512,256]{1,2,0:T(8,128)}, f32[1,256,512]{1,2,0:T(8,128)}), (f32[1,256,512]{1,2,0:T(8,128)}, f32[1,512,256]{1,2,0:T(8,128)}, f32[1,256,512]{1,2,0:T(8,128)})) %all-reduce.7.cloned.1.call-update) | async-done | bytes 1572880 | tf_op jit(solution)/shard_map/psum | solution.py:62
  305.0 1.9 convolution_bitcast_fusion.7
  306.9 0.0 copy-start.14
  306.9 0.5 convolution_bitcast_fusion.9
  307.3 0.5 copy-done.4
  307.9 0.1 copy-done.14
  308.0 0.7 convolution_bitcast_fusion.8
  308.7 0.0 copy-start.11
  308.7 1.4 convolution_bitcast_fusion.1
  310.1 1.4 fusion.60
  311.6 1.4 convolution_bitcast_fusion
  313.0 0.0 all-reduce.5.cloned.1.call-update
  313.1 0.0 copy-start.27
  313.1 2.4 fusion.18
  315.5 0.0 copy-start.12
  315.5 0.7 fusion.2
  316.1 0.4 copy-done.7
  316.5 0.1 copy-done.12
  316.6 0.5 fusion.4
  317.1 0.5 copy-done.5
  317.6 0.5 fusion.1
  318.1 0.7 maximum_bitcast_fusion
  318.8 274.7 %all-reduce.5.cloned.1.call-done = (f32[256,512]{0,1:T(8,128)}, f32[512,256]{1,0:T(8,128)}, f32[256,512]{0,1:T(8,128)}) async-done(((f32[256,512]{0,1:T(8,128)}, f32[512,256]{1,0:T(8,128)}, f32[256,512]{0,1:T(8,128)}), (f32[256,512]{0,1:T(8,128)}, f32[512,256]{1,0:T(8,128)}, f32[256,512]{0,1:T(8,128)})) %all-reduce.5.cloned.1.call-update) | async-done | bytes 1572880 | tf_op jit(solution)/shard_map/psum | solution.py:70
  593.5 1.8 convolution_bitcast_fusion.5
  595.3 0.0 copy-start.9
  595.3 0.5 fusion.63
  595.8 0.4 copy-done.9
  596.2 0.2 copy-done.17
  596.4 0.7 fusion.86
  597.1 0.7 convolution_bitcast_fusion.6
  597.8 0.7 convolution_add_fusion.3
  598.5 0.2 copy-done.20
  598.7 0.5 convolution_add_fusion.2
  599.2 0.5 fusion.16
  599.8 1.5 convolution_add_fusion.1
  601.2 1.1 fusion.3
  (32 shorter events, 0.1 us)
Async XLA Ops:
  7.2 0.9 copy-start
  7.2 2.4 copy-start.1
  7.2 297.8 %all-reduce.7.cloned.1.call-start = ((), (), s32[]{:S(2)}) async-start(), calls=%async_computation.1 | async-start | bytes 3145728 | tf_op jit(solution)/shard_map/psum | solution.py:62
  9.6 1.0 copy-start.2
  9.6 1.1 copy-start.8
  10.0 2.9 copy-start.19
  10.0 0.7 copy-start.26
  15.8 0.9 copy-start.23
  15.8 1.6 copy-start.3
  15.8 577.6 %all-reduce.5.cloned.1.call-start = ((), (), s32[]{:S(2)}) async-start(), calls=%async_computation | async-start | bytes 3145728 | tf_op jit(solution)/shard_map/psum | solution.py:70
  18.6 0.9 copy-start.13
  20.0 1.2 copy-start.21
  304.9 1.9 copy-start.6
  304.9 1.9 copy-start.18
  305.0 1.9 copy-start.24
  306.9 1.0 copy-start.4
  306.9 1.1 copy-start.14
  308.7 2.9 copy-start.11
  313.0 2.4 copy-start.22
  313.1 2.4 copy-start.25
  313.1 2.4 copy-start.27
  315.4 1.0 copy-start.7
  315.5 1.1 copy-start.12
  316.5 1.0 copy-start.5
  593.5 1.8 copy-start.16
  593.5 1.8 copy-start.10
  595.3 0.9 copy-start.9
  595.3 1.1 copy-start.17
  595.8 1.3 copy-start.15
  597.8 1.0 copy-start.20
Sparse Core Ops, SparseCore 0:
  15.9 288.9 all-reduce.6
  313.2 280.2 all-reduce.4
where the time goes:
time: 610 us; the launch traced here: 609 us
  waiting for transfers between devices  557 us (91%)
  matrix products  29.7 us (5%)
  between operations  14.4 us (2%)
  local copies, waits for them, and re-layouts  6.9 us (1%)
    psum x1, waiting for transfers between devices, body(): totals = lax.psum((inner[0], inner[1], inner[2]), 'ctx')  282 us
    psum x1, waiting for transfers between devices, body(): direction = lax.psum((wg_local, wu_local, down_local), 'ctx')  275 us
  transfers between devices with their start and end apart: 2, of which 2 were waited for; matrix products, arithmetic and copies ran while one was open for 2% of the time, Pallas kernels for 0%

commit v1 on v0

v1 whole, which is shorter than its diff:
```python
import functools

import jax
import jax.numpy as jnp
from jax import lax
from jax.experimental import pallas as pl
from jax.experimental.pallas import tpu as pltpu
from jax.sharding import Mesh
from jax.sharding import PartitionSpec as P

NX, NC = 4, 2
NN = ((1,), (0,))
NT = ((1,), (1,))
MIB = 1 << 20
LANES = 128


def split(a):
    head = a.astype(jnp.bfloat16)
    tail = (a - head.astype(jnp.float32)).astype(jnp.bfloat16)
    return head, tail


def dot3(a, b, dims):
    rows = a[0].shape[0]
    dot = functools.partial(
        lax.dot_general, dimension_numbers=(dims, ((), ())), preferred_element_type=jnp.float32
    )
    both = dot(jnp.concatenate(a, axis=0), b[0])
    return both[:rows] + (both[rows:] + dot(a[0], b[1]))


def gates(gate):
    sigma = jax.nn.sigmoid(gate)
    return sigma, gate * sigma, sigma * (1.0 + gate * (1.0 - sigma))


def call(kernel, shapes, flops, n_bytes, limit=16, **more):
    return pl.pallas_call(
        kernel,
        out_shape=shapes,
        **more,
        compiler_params=pltpu.CompilerParams(vmem_limit_bytes=limit * MIB),
        cost_estimate=pl.CostEstimate(flops=flops, bytes_accessed=n_bytes, transcendentals=0),
    )


def start_all(pairs, sems):
    copies = [pltpu.make_async_copy(*pair, sems.at[i]) for i, pair in enumerate(pairs)]
    for copy in copies:
        copy.start()
    return copies


def pack_kernel(k_ref, v_ref, r_ref, inner_ref, rate_ref, raw_ref, row_ref, sems):
    width = k_ref.shape[1]
    tok = r_ref.shape[1]
    copies = start_all([(r_ref, row_ref), (v_ref, raw_ref), (k_ref, inner_ref.at[:, :width])], sems)
    copies[0].wait()
    rate = jnp.broadcast_to(row_ref[...], (LANES, tok)).T
    rate_ref[...] = rate
    copies[1].wait()
    for at in range(0, width, LANES):
        inner_ref[:, width + at : width + at + LANES] = rate * raw_ref[:, at : at + LANES]
    copies[2].wait()


def units_kernel(wg_ref, wu_ref, wd_ref, q_ref, c_ref, out_ref, ask_ref, raw_ref, sems):
    nx, rows, width = out_ref.shape
    units = rows // 3
    half = nx * units
    start = pl.multiple_of(lax.axis_index("c") * half, LANES)
    pairs = [
        (wg_ref.at[0, :, pl.ds(start, half)], raw_ref.at[0]),
        (wu_ref.at[0, :, pl.ds(start, half)], raw_ref.at[1]),
    ]
    pairs += [(wd_ref.at[0, pl.ds(start + i * units, units)], out_ref.at[i, 2 * units :]) for i in range(nx)]
    tok = q_ref.shape[1]
    copies = start_all(pairs + [(q_ref.at[1], ask_ref.at[:tok]), (c_ref.at[1], ask_ref.at[tok:])], sems)
    for i in range(2):
        copies[i].wait()
        out_ref[:, i * units : (i + 1) * units] = raw_ref[i].T.reshape(nx, units, width)
    for copy in copies[2:]:
        copy.wait()


def row_sum_kernel(in_ref, out_ref, ask_ref):
    nx = in_ref.shape[0]
    rows = out_ref.shape[0]
    tok = ask_ref.shape[1] // nx
    total = in_ref[0, :rows]
    for i in range(1, nx):
        total += in_ref[i, :rows]
    out_ref[...] = total
    for i in range(nx):
        for j in range(2):
            ask_ref[j, i * tok : (i + 1) * tok] = in_ref[i, rows + j * tok : rows + (j + 1) * tok]


def update_kernel(scale, in_ref, w_ref, out_ref):
    n = in_ref.shape[0]
    total = in_ref[0]
    for i in range(1, n):
        total += in_ref[i]
    total = w_ref[...] + scale * total
    for i in range(n):
        out_ref[i] = total


def total_kernel(in_ref, out_ref):
    n = in_ref.shape[0]
    total = in_ref[0]
    for i in range(1, n):
        total += in_ref[i]
    for i in range(n):
        out_ref[i] = total


def parts(ref, units):
    width = ref.shape[2]
    return [ref[:, i * units : (i + 1) * units].reshape(-1, width) for i in range(3)]


def weight_grad(w_in, w_down, chunks):
    n = w_down[0].shape[0]
    total = None
    for rows, cots in chunks:
        rows, cots = split(rows), split(cots)
        both = dot3(w_in, rows, NT)
        hidden_grad = dot3(w_down, cots, NT)
        up_part = both[n:]
        _, active, slope = gates(both[:n])
        in_grad = jnp.concatenate([hidden_grad * up_part * slope, hidden_grad * active], axis=0)
        new = dot3(split(in_grad), rows, NN), dot3(split(active * up_part), cots, NN)
        total = new if total is None else (total[0] + new[0], total[1] + new[1])
    return total


def inner_kernel(own_ref, other_ref, ask_ref, w_ref, out_ref, piece_ref, pair_ref, kept_ref, sems):
    nx, rows, width = w_ref.shape
    units = rows // 3
    n = nx * units
    tok = own_ref.shape[0]
    copies = start_all([(own_ref, pair_ref.at[:tok]), (other_ref, pair_ref.at[tok:]), (w_ref, kept_ref)], sems)
    piece = piece_ref.shape[0]
    start = pl.multiple_of(lax.axis_index("z") * piece, 8)
    piece_ref[...] = w_ref[lax.axis_index("x"), pl.ds(start, piece)]
    w_gate, w_up, w_down = parts(w_ref, units)
    pair = jnp.concatenate([own_ref[...], other_ref[...]], axis=0)
    in_sum, down_sum = weight_grad(
        split(jnp.concatenate([w_gate, w_up], axis=0)), split(w_down), [(pair[:, :width], pair[:, width:])]
    )
    out_ref[:, :units] = in_sum[:n].reshape(nx, units, width)
    out_ref[:, units : 2 * units] = in_sum[n:].reshape(nx, units, width)
    out_ref[:, 2 * units : rows] = down_sum.reshape(nx, units, width)
    for i in range(nx):
        out_ref[i, rows:] = ask_ref[...]
    for copy in copies:
        copy.wait()


def outer_kernel(ask_ref, got_ref, w_ref, out_ref, pair_ref, sems):
    width = w_ref.shape[1]
    units = w_ref.shape[0] // 3
    tok = pair_ref.shape[0] // 2
    at = pl.ds(pl.multiple_of(lax.axis_index("x") * tok, 8), tok)
    copies = start_all(
        [
            (ask_ref.at[0, at], pair_ref.at[:tok, :width]),
            (ask_ref.at[1, at], pair_ref.at[:tok, width:]),
            (got_ref.at[0, at], pair_ref.at[tok:, :width]),
            (got_ref.at[1, at], pair_ref.at[tok:, width:]),
        ],
        sems,
    )
    step = 256
    chunks = [
        (ref[0, at : at + step], ref[1, at : at + step])
        for ref in (ask_ref, got_ref)
        for at in range(0, ref.shape[1], step)
    ]
    in_sum, down_sum = weight_grad(split(w_ref[: 2 * units]), split(w_ref[2 * units :]), chunks)
    out_ref[: 2 * units] = in_sum
    out_ref[2 * units :] = down_sum
    for copy in copies:
        copy.wait()


def query_grad(rows, cots, w_gate, w_up, w_down, up_way, down_way):
    rows, cots = split(rows), split(cots)
    gate, up_part = dot3(rows, w_gate, up_way), dot3(rows, w_up, up_way)
    hidden_grad = dot3(cots, w_down, NT)
    _, active, slope = gates(gate)
    return dot3(split(hidden_grad * up_part * slope), w_gate, down_way) + dot3(
        split(hidden_grad * active), w_up, down_way
    )


def query_kernel(q_ref, c_ref, wg_ref, wu_ref, wd_ref, pair_ref, w_ref, zero_ref, mine_ref, theirs_ref):
    tok, width = zero_ref.shape
    zero_ref[...] = query_grad(
        q_ref[0], c_ref[0], split(wg_ref[0]), split(wu_ref[0]), split(wd_ref[0]), NN, NT
    )
    w_gate, w_up, w_down = [split(w) for w in parts(w_ref, w_ref.shape[1] // 3)]
    grad = query_grad(pair_ref[:, :width], pair_ref[:, width:], w_gate, w_up, w_down, NT, NN)
    mine_ref[...] = grad[:tok]
    theirs_ref[...] = grad[tok:]


def final_kernel(d_ref, pair_ref, w_ref, query_ref, mine_ref, theirs_ref):
    width = d_ref.shape[2]
    units = d_ref.shape[1] // 3
    w_gate, w_up, w_down = [split(w) for w in parts(w_ref, units)]
    rows, cots = split(pair_ref[:, :width]), split(pair_ref[:, width:])
    gate, up_part = dot3(rows, w_gate, NT), dot3(rows, w_up, NT)
    hidden_grad = dot3(cots, w_down, NT)
    sigma, active, slope = gates(gate)
    bend = sigma * (1.0 - sigma) * (2.0 + gate * (1.0 - 2.0 * sigma))
    steep = slope * up_part
    d_gate, d_up, d_down = [split(d) for d in parts(d_ref, units)]
    d_g, d_u = dot3(rows, d_gate, NT), dot3(rows, d_up, NT)
    d_c = dot3(cots, d_down, NT)
    d_h = steep * d_g + active * d_u
    value = dot3(split(active * up_part), d_down, NN) + dot3(split(d_h), w_down, NN)
    to_gate = hidden_grad * (up_part * bend * d_g + slope * d_u) + steep * d_c
    to_up = hidden_grad * slope * d_g + active * d_c
    key = (
        dot3(split(hidden_grad * steep), d_gate, NN)
        + dot3(split(hidden_grad * active), d_up, NN)
        + dot3(split(to_gate), w_gate, NN)
        + dot3(split(to_up), w_up, NN)
    )
    tok = mine_ref.shape[0]
    mine_ref[:, :width] = key[:tok]
    mine_ref[:, width:] = value[:tok]
    theirs_ref[:, :width] = key[tok:]
    theirs_ref[:, width : 2 * width] = value[tok:]
    theirs_ref[:, 2 * width :] = query_ref[...]


def join_kernel(scale, mine_ref, got_ref, rate_ref, zero_ref, one_ref, q_ref, k_ref, v_ref):
    width = k_ref.shape[1]
    q_ref[0] = zero_ref[...]
    q_ref[1] = one_ref[...] + got_ref[:, 2 * width :]
    k_ref[...] = scale * (mine_ref[:, :width] + got_ref[:, :width])
    rate = scale * rate_ref[...]
    for at in range(0, width, LANES):
        lanes = slice(width + at, width + at + LANES)
        v_ref[:, at : at + LANES] = rate * (mine_ref[:, lanes] + got_ref[:, lanes])


def after(value, *others):
    return lax.optimization_barrier((value, others))[0]


def both(*values):
    return lax.optimization_barrier(values)


def body(queries, keys, values, rates, grad_out, w_gate, w_up, w_down):
    tok, width = keys.shape
    hidden = w_gate.shape[2]
    n_z = lax.axis_size("z")
    units = hidden // (NX * NC)
    half = NX * units
    piece = 3 * units // n_z
    scale = float(tok * NX * NC * n_z) ** (-0.5)
    f32 = lambda *shape: jax.ShapeDtypeStruct(shape, jnp.float32)
    swap = lambda x: lax.ppermute(x, "c", [(i, (i + 1) % NC) for i in range(NC)])
    gather = lambda x: lax.all_gather(x, "x", axis=0, tiled=True)
    exchange = lambda x: lax.all_to_all(x.reshape(n_z, piece, width), "z", 0, 0)
    hold = lambda x: pltpu.with_memory_space_constraint(x, pltpu.HBM)
    n_mul = 2 * tok * width * half
    n_w = 12 * width * half
    here, there = pl.BlockSpec(memory_space=pltpu.VMEM), pl.BlockSpec(memory_space=pltpu.HBM)

    own, rate = call(
        pack_kernel,
        [f32(tok, 2 * width), f32(tok, LANES)],
        0,
        16 * tok * width,
        in_specs=[there] * 3,
        out_specs=[here] * 2,
        scratch_shapes=[
            pltpu.VMEM((tok, width), jnp.float32), pltpu.VMEM((1, tok), jnp.float32), pltpu.SemaphoreType.DMA((3,))
        ],
    )(hold(keys), hold(values), hold(rates.reshape(1, tok)))
    other = swap(own)
    w_rows, ask = call(
        units_kernel,
        [f32(NX, 3 * units, width), f32(2 * tok, width)],
        0,
        2 * n_w,
        in_specs=[there] * 5,
        out_specs=[here] * 2,
        scratch_shapes=[pltpu.VMEM((2, width, half), jnp.float32), pltpu.SemaphoreType.DMA((4 + NX,))],
    )(hold(w_gate), hold(w_up), hold(w_down), hold(queries), hold(grad_out))

    pair_shape = pltpu.HBM((2 * tok, 2 * width), jnp.float32)
    kept_shape = pltpu.HBM((NX, 3 * units, width), jnp.float32)
    inner, w_piece, pair, kept = call(
        inner_kernel,
        [f32(NX, 3 * units + 2 * tok, width), f32(piece, width), pair_shape, kept_shape],
        36 * n_mul,
        2 * n_w,
        in_specs=[here] * 4,
        out_specs=[here, here, there, there],
        scratch_shapes=[pltpu.SemaphoreType.DMA((3,))],
    )(own, other, ask, w_rows)
    inner = lax.all_to_all(inner, "x", 0, 0)
    inner, ask = call(row_sum_kernel, [f32(3 * units, width), f32(2, NX * tok, width)], 0, 4 * n_w)(inner)
    pieces = f32(n_z, piece, width)
    new = call(functools.partial(update_kernel, scale), pieces, 0, n_w)(exchange(inner), w_piece)
    ask_got = swap(after(ask, new))
    new, ask_got = both(exchange(new).reshape(3 * units, width), ask_got)

    outer, asked = call(
        outer_kernel,
        [f32(3 * units, width), pair_shape],
        36 * n_mul,
        64 * tok * width,
        in_specs=[here] * 3,
        out_specs=[here, there],
        scratch_shapes=[pltpu.SemaphoreType.DMA((4,))],
    )(ask, ask_got, new)
    got, new_x = both(exchange(outer), gather(after(new, outer)))
    outer = call(total_kernel, pieces, 0, n_w)(got)
    new_x = after(new_x, outer).reshape(NX, 3 * units, width)
    zero, one, one_theirs = call(query_kernel, [f32(tok, width)] * 3, 60 * n_mul, 4 * n_w)(
        queries, grad_out, w_gate, w_up, w_down, asked, new_x
    )
    outer, one_theirs = both(exchange(outer).reshape(3 * units, width), one_theirs)
    d_all = gather(outer).reshape(NX, 3 * units, width)
    mine, theirs = call(
        final_kernel, [f32(tok, 2 * width), f32(tok, 3 * width)], 72 * n_mul, 3 * n_w
    )(d_all, pair, kept, one_theirs)
    return call(
        functools.partial(join_kernel, scale), [f32(2, tok, width), f32(tok, width), f32(tok, width)], 0, 40 * tok * width
    )(mine, swap(theirs), rate, zero, one)


def solution(mesh):
    devices = mesh.devices.reshape(-1, NX, NC, mesh.devices.shape[1])
    fine = Mesh(devices, ("z", "x", "c", "head"))
    ctx = ("z", "x", "c")
    in_specs = (
        P(None, ctx, "head"),
        P(ctx, "head"),
        P(ctx, "head"),
        P(ctx, "head"),
        P(None, ctx, "head"),
        P("head", None, None),
        P("head", None, None),
        P("head", None, None),
    )
    out_specs = (P(None, ctx, "head"), P(ctx, "head"), P(ctx, "head"))
    return jax.shard_map(body, mesh=fine, in_specs=in_specs, out_specs=out_specs, check_vma=False)
```

time: 610 us -> 150 us (0.25)
  waiting for transfers between devices: 557 us -> 9.8 us
  blocking collectives: 0 us -> 84.1 us
  starting transfers between devices: 0.26 us -> 39.9 us
  matrix products: 29.7 us -> 0 us
  between operations: 14.4 us -> 0.81 us
  Pallas kernels: 0 us -> 11.1 us
    psum x2 -> x0, waiting for transfers between devices: 557 us -> none  [the longest x1 282 us: body(): totals = lax.psum((inner[0], inner[1], inner[2]), 'ctx')]
    all_to_all x0 -> x3, blocking collectives: none -> 60 us  [the longest x2 34.3 us: body(): exchange = lambda x: lax.all_to_all(x.reshape(n_z, piece, width), 'z', 0, 0)]
    dot_general x29 -> x0, matrix products: 29.7 us -> none  [the longest x7 7.45 us: apply_fast(): return jnp.dot(jax.nn.silu(gate) * up_part, w_down, precision=best)]
    ppermute x0 -> x3, starting transfers between devices: none -> 27.2 us  [body(): lax.ppermute(x, 'c', [(i, (i + 1) % NC) for i in range(NC)])]
    all_gather x0 -> x2, blocking collectives: none -> 24.1 us  [body(): gather = lambda x: lax.all_gather(x, 'x', axis=0, tiled=True)]
    all_to_all x0 -> x2, starting transfers between devices: none -> 12.7 us  [body(): exchange = lambda x: lax.all_to_all(x.reshape(n_z, piece, width), 'z', 0, 0)]
    pallas_call x0 -> x10, Pallas kernels: none -> 11.1 us  [the longest x1 2.54 us: body(): call(outer_kernel, [f32(3 * units, width), pair_shape], 36 * n_mul, 64 *...]
    all_to_all x0 -> x2, waiting for transfers between devices: none -> 8.47 us  [body(): exchange = lambda x: lax.all_to_all(x.reshape(n_z, piece, width), 'z', 0, 0)]
  transfers between devices with their start and end apart: 2 -> 5, of which waited for: 2 -> 2; matrix products, arithmetic and copies ran while one was open for 2% -> 0% of each run, Pallas kernels for 0% -> 2%
where the time goes in v1:
time: 150 us; the launch traced here: 149 us
  blocking collectives  84.1 us (56%)
  starting transfers between devices  39.9 us (27%)
  Pallas kernels  11.1 us (7%)
  waiting for transfers between devices  9.8 us (7%)
  local copies, waits for them, and re-layouts  3.23 us (2%)
    all_to_all x2, blocking collectives, body(): exchange = lambda x: lax.all_to_all(x.reshape(n_z, piece, width), 'z', 0, 0)  34.3 us
    ppermute x3, starting transfers between devices, body(): lax.ppermute(x, 'c', [(i, (i + 1) % NC) for i in range(NC)])  27.2 us
    all_to_all x1, blocking collectives, body(): inner = lax.all_to_all(inner, 'x', 0, 0)  25.7 us
    all_gather x2, blocking collectives, body(): gather = lambda x: lax.all_gather(x, 'x', axis=0, tiled=True)  24.1 us
    all_to_all x2, starting transfers between devices, body(): exchange = lambda x: lax.all_to_all(x.reshape(n_z, piece, width), 'z', 0, 0)  12.7 us
    all_to_all x2, waiting for transfers between devices, body(): exchange = lambda x: lax.all_to_all(x.reshape(n_z, piece, width), 'z', 0, 0)  8.47 us
    unnamed x16, local copies, waits for them, and re-layouts  3.23 us
  transfers between devices with their start and end apart: 5, of which 2 were waited for; matrix products, arithmetic and copies ran while one was open for 0% of the time, Pallas kernels for 2%

profile of v1, /device:TPU:1, one launch (start us, length us, event | category | flops | bytes accessed | tf_op | source)
XLA Modules:
  0.0 149.0 jit_solution(11437958329055609712)
XLA Ops:
  0.6 1.0 shard_map.103
  1.6 12.4 %collective-permute-start = (f32[128,512]{1,0:T(8,128)S(1)}, f32[128,512]{1,0:T(8,128)S(1)}, u32[]{:S(2)}, u32[]{:S(2)}) collective-permute-start(f32[128,512]{1,0:T(8,128)S(1)} %get-tuple-element.29.own_ref), channel_id=1, source_target_pairs={{0,8},{8,0},{1,9},{9,1},{2,10},{10,2},{3,11},{11,3},{4,12},{12,4},... | collective-permute-start | bytes 786440 | tf_op jit(solution)/shard_map/ppermute | solution.py:269
  14.1 1.3 shard_map.104
  15.4 0.0 collective-permute-done.other_ref
  15.4 1.1 shard_map.105
  16.6 25.7 %all_to_all.25.in_ref = f32[4,448,256]{2,1,0:T(8,128)S(1)} all-to-all(f32[4,448,256]{2,1,0:T(8,128)S(1)} %get-tuple-element.32), channel_id=1, replica_groups=mesh['z'=12,'x'=4,'c'=2,'head'=8] {'x'}, dimensions={0} | all-to-all | bytes 3670016 | tf_op jit(solution)/shard_map/all_to_all | solution.py:310
  42.3 0.1 shard_map.106
  42.4 18.5 %all_to_all.26.in_ref = f32[12,16,256]{2,1,0:T(8,128)S(1)} all-to-all(f32[12,16,256]{2,1,0:T(8,128)S(1)} %bitcast.11), channel_id=1, replica_groups=mesh['z'=12,'x'=4,'c'=2,'head'=8] {'z'}, dimensions={0} | all-to-all | bytes 393216 | tf_op jit(solution)/shard_map/all_to_all | solution.py:271
  60.9 5.2 %collective-permute-start.1 = (f32[2,512,256]{2,1,0:T(8,128)S(1)}, f32[2,512,256]{2,1,0:T(8,128)S(1)}, u32[]{:S(2)}, u32[]{:S(2)}) collective-permute-start(f32[2,512,256]{2,1,0:T(8,128)S(1)} %get-tuple-element.36.ask_ref), channel_id=1, source_target_pairs={{0,8},{8,0},{1,9},{9,1},{2,10},{10,2},{3,11},{11,3},{4,12},{12,4},... | collective-permute-start | bytes 3145736 | tf_op jit(solution)/shard_map/ppermute | solution.py:269
  66.2 15.8 %all_to_all.27 = f32[12,16,256]{2,1,0:T(8,128)S(1)} all-to-all(f32[12,16,256]{2,1,0:T(8,128)S(1)} %shard_map.107), channel_id=1, replica_groups=mesh['z'=12,'x'=4,'c'=2,'head'=8] {'z'}, dimensions={0} | all-to-all | bytes 393216 | tf_op jit(solution)/shard_map/all_to_all | solution.py:271
  82.0 0.0 collective-permute-done.1.got_ref
  82.0 0.0 copy-start
  82.0 0.0 copy-start.1
  82.0 0.0 copy-start.2
  82.0 0.0 copy-start.3
  82.0 0.0 copy-start.4
  82.0 2.5 %shard_map.108 = (f32[192,256]{1,0:T(8,128)}, f32[256,512]{1,0:T(8,128)}) custom-call(f32[2,512,256]{2,1,0:T(8,128)S(1)} %get-tuple-element.36.ask_ref, f32[2,512,256]{2,1,0:T(8,128)S(1)} %collective-permute-done.1.got_ref, f32[192,256]{1,0:T(8,128)S(1)} %bitcast.7), custom_call_target="tpu_custom_call" | custom-call | flops 603979776 | bytes 2097152 | tf_op jit(solution)/shard_map/pallas_call | solution.py:317
  84.6 3.6 %all-to-all-start.3 = ((f32[12,16,256]{2,1,0:T(8,128)}), f32[12,16,256]{2,1,0:T(8,128)S(1)}, u32[]{:S(2)}, u32[]{:S(2)}) async-start(f32[12,16,256]{2,1,0:T(8,128)} %bitcast.3), calls=%async_computation.3 | async-start | bytes 393216 | tf_op jit(solution)/shard_map/all_to_all | solution.py:271
  88.2 12.2 %all_gather.6 = f32[768,256]{1,0:T(8,128)S(1)} all-gather(f32[192,256]{1,0:T(8,128)S(1)} %bitcast.8), channel_id=1, replica_groups=mesh['z'=12,'x'=4,'c'=2,'head'=8] {'x'}, dimensions={0}, use_global_device_ids=true | all-gather | bytes 983040 | tf_op jit(solution)/shard_map/all_gather | solution.py:270
  100.4 0.0 all-to-all-done.3.in_ref
  100.4 0.7 shard_map.109
  101.1 9.1 %all-to-all-start.4 = ((f32[12,16,256]{2,1,0:T(8,128)}), f32[12,16,256]{2,1,0:T(8,128)}, u32[]{:S(2)}, u32[]{:S(2)}) async-start(f32[12,16,256]{2,1,0:T(8,128)} %shard_map.109), calls=%async_computation.4 | async-start | bytes 393216 | tf_op jit(solution)/shard_map/all_to_all | solution.py:271
  110.2 0.0 copy-done
  110.2 0.0 copy-done.1
  110.2 0.0 copy-done.2
  110.2 0.0 copy-done.3
  110.2 0.0 copy-done.4
  110.2 0.0 copy-start.5
  110.3 1.0 copy-done.5
  111.3 1.6 %shard_map.110 = (f32[128,256]{1,0:T(8,128)S(1)}, f32[128,256]{1,0:T(8,128)S(1)}, f32[128,256]{1,0:T(8,128)S(1)}) custom-call(f32[2,128,256]{2,1,0:T(8,128)S(1)} %copy-done.3, f32[2,128,256]{2,1,0:T(8,128)S(1)} %copy-done.4, f32[1,256,512]{2,1,0:T(8,128)S(1)} %copy-done, f32[1,256,512]{2,1,0:T(8,128)S(1)} %copy-done.1, f32[1,512,256]{2,1,0:T(8,128)S(1)} %copy-done.2, ...), custom_call_target="tpu_custom_call" | custom-call | flops 1006632960 | bytes 3145728 | tf_op jit(solution)/shard_map/pallas_call | solution.py:329
  112.9 8.5 %all-to-all-done.4 = f32[12,16,256]{2,1,0:T(8,128)} async-done(((f32[12,16,256]{2,1,0:T(8,128)}), f32[12,16,256]{2,1,0:T(8,128)}, u32[]{:S(2)}, u32[]{:S(2)}) %all-to-all-start.4) | async-done | bytes 196640 | tf_op jit(solution)/shard_map/all_to_all | solution.py:271
  121.4 11.9 %all_gather.7 = f32[768,256]{1,0:T(8,128)S(1)} all-gather(f32[192,256]{1,0:T(8,128)} %bitcast.4), channel_id=1, replica_groups=mesh['z'=12,'x'=4,'c'=2,'head'=8] {'x'}, dimensions={0}, use_global_device_ids=true | all-gather | bytes 983040 | tf_op jit(solution)/shard_map/all_gather | solution.py:270
  133.3 0.0 copy-start.6
  133.3 1.1 copy-done.6
  134.5 0.0 copy-start.7
  134.5 1.0 copy-done.7
  135.5 1.8 %shard_map.111 = (f32[128,512]{1,0:T(8,128)S(1)}, f32[128,768]{1,0:T(8,128)S(1)}) custom-call(f32[4,192,256]{2,1,0:T(8,128)S(1)} %bitcast.10, f32[256,512]{1,0:T(8,128)S(1)} %copy-done.7, f32[4,192,256]{2,1,0:T(8,128)S(1)} %copy-done.6, f32[128,256]{1,0:T(8,128)S(1)} %get-tuple-element.49.query_ref), custom_call_target="tpu_custom_call" | custom-call | flops 1207959552 | bytes 2359296 | tf_op jit(solution)/shard_map/pallas_call | solution.py:334
  137.3 9.6 %collective-permute-start.2 = (f32[128,768]{1,0:T(8,128)S(1)}, f32[128,768]{1,0:T(8,128)S(1)}, u32[]{:S(2)}, u32[]{:S(2)}) collective-permute-start(f32[128,768]{1,0:T(8,128)S(1)} %get-tuple-element.51), channel_id=1, source_target_pairs={{0,8},{8,0},{1,9},{9,1},{2,10},{10,2},{3,11},{11,3},{4,12},{12,4},... | collective-permute-start | bytes 1179656 | tf_op jit(solution)/shard_map/ppermute | solution.py:269
  146.9 1.3 collective-permute-done.2.got_ref
  148.2 0.8 shard_map.112
  (1 shorter events, 0.0 us)
Async XLA Ops:
  1.6 13.8 %collective-permute-start = (f32[128,512]{1,0:T(8,128)S(1)}, f32[128,512]{1,0:T(8,128)S(1)}, u32[]{:S(2)}, u32[]{:S(2)}) collective-permute-start(f32[128,512]{1,0:T(8,128)S(1)} %get-tuple-element.29.own_ref), channel_id=1, source_target_pairs={{0,8},{8,0},{1,9},{9,1},{2,10},{10,2},{3,11},{11,3},{4,12},{12,4},... | collective-permute-start | bytes 786440 | tf_op jit(solution)/shard_map/ppermute | solution.py:269
  60.9 21.1 %collective-permute-start.1 = (f32[2,512,256]{2,1,0:T(8,128)S(1)}, f32[2,512,256]{2,1,0:T(8,128)S(1)}, u32[]{:S(2)}, u32[]{:S(2)}) collective-permute-start(f32[2,512,256]{2,1,0:T(8,128)S(1)} %get-tuple-element.36.ask_ref), channel_id=1, source_target_pairs={{0,8},{8,0},{1,9},{9,1},{2,10},{10,2},{3,11},{11,3},{4,12},{12,4},... | collective-permute-start | bytes 3145736 | tf_op jit(solution)/shard_map/ppermute | solution.py:269
  82.0 28.2 %copy-start = (f32[1,256,512]{2,1,0:T(8,128)S(1)}, f32[1,256,512]{2,1,0:T(8,128)}, u32[]{:S(2)}) copy-start(f32[1,256,512]{2,1,0:T(8,128)} %wg_ref.3) | copy-start | bytes 1572868
  82.0 28.2 %copy-start.1 = (f32[1,256,512]{2,1,0:T(8,128)S(1)}, f32[1,256,512]{2,1,0:T(8,128)}, u32[]{:S(2)}) copy-start(f32[1,256,512]{2,1,0:T(8,128)} %wu_ref.3) | copy-start | bytes 1572868
  82.0 28.2 %copy-start.2 = (f32[1,512,256]{2,1,0:T(8,128)S(1)}, f32[1,512,256]{2,1,0:T(8,128)}, u32[]{:S(2)}) copy-start(f32[1,512,256]{2,1,0:T(8,128)} %wd_ref.3) | copy-start | bytes 1572868
  82.0 28.2 %copy-start.3 = (f32[2,128,256]{2,1,0:T(8,128)S(1)}, f32[2,128,256]{2,1,0:T(8,128)}, u32[]{:S(2)}) copy-start(f32[2,128,256]{2,1,0:T(8,128)} %q_ref.3) | copy-start | bytes 786436
  82.0 28.2 %copy-start.4 = (f32[2,128,256]{2,1,0:T(8,128)S(1)}, f32[2,128,256]{2,1,0:T(8,128)}, u32[]{:S(2)}) copy-start(f32[2,128,256]{2,1,0:T(8,128)} %c_ref.3) | copy-start | bytes 786436
  84.6 15.8 %all-to-all-start.3 = ((f32[12,16,256]{2,1,0:T(8,128)}), f32[12,16,256]{2,1,0:T(8,128)S(1)}, u32[]{:S(2)}, u32[]{:S(2)}) async-start(f32[12,16,256]{2,1,0:T(8,128)} %bitcast.3), calls=%async_computation.3 | async-start | bytes 393216 | tf_op jit(solution)/shard_map/all_to_all | solution.py:271
  101.1 20.3 %all-to-all-start.4 = ((f32[12,16,256]{2,1,0:T(8,128)}), f32[12,16,256]{2,1,0:T(8,128)}, u32[]{:S(2)}, u32[]{:S(2)}) async-start(f32[12,16,256]{2,1,0:T(8,128)} %shard_map.109), calls=%async_computation.4 | async-start | bytes 393216 | tf_op jit(solution)/shard_map/all_to_all | solution.py:271
  110.2 1.0 copy-start.5
  133.3 1.1 copy-start.6
  134.5 1.0 copy-start.7
  137.3 10.9 %collective-permute-start.2 = (f32[128,768]{1,0:T(8,128)S(1)}, f32[128,768]{1,0:T(8,128)S(1)}, u32[]{:S(2)}, u32[]{:S(2)}) collective-permute-start(f32[128,768]{1,0:T(8,128)S(1)} %get-tuple-element.51), channel_id=1, source_target_pairs={{0,8},{8,0},{1,9},{9,1},{2,10},{10,2},{3,11},{11,3},{4,12},{12,4},... | collective-permute-start | bytes 1179656 | tf_op jit(solution)/shard_map/ppermute | solution.py:269

commit v2 on v1

--- a/solution.py
+++ b/solution.py
@@ -65,7 +65,7 @@
     copies[2].wait()
 
 
-def units_kernel(wg_ref, wu_ref, wd_ref, q_ref, c_ref, out_ref, ask_ref, raw_ref, sems):
+def units_kernel(wg_ref, wu_ref, wd_ref, out_ref, raw_ref, sems):
     nx, rows, width = out_ref.shape
     units = rows // 3
     half = nx * units
@@ -75,8 +75,7 @@
         (wu_ref.at[0, :, pl.ds(start, half)], raw_ref.at[1]),
     ]
     pairs += [(wd_ref.at[0, pl.ds(start + i * units, units)], out_ref.at[i, 2 * units :]) for i in range(nx)]
-    tok = q_ref.shape[1]
-    copies = start_all(pairs + [(q_ref.at[1], ask_ref.at[:tok]), (c_ref.at[1], ask_ref.at[tok:])], sems)
+    copies = start_all(pairs, sems)
     for i in range(2):
         copies[i].wait()
         out_ref[:, i * units : (i + 1) * units] = raw_ref[i].T.reshape(nx, units, width)
@@ -84,17 +83,11 @@
         copy.wait()
 
 
-def row_sum_kernel(in_ref, out_ref, ask_ref):
-    nx = in_ref.shape[0]
-    rows = out_ref.shape[0]
-    tok = ask_ref.shape[1] // nx
-    total = in_ref[0, :rows]
-    for i in range(1, nx):
-        total += in_ref[i, :rows]
+def row_sum_kernel(in_ref, out_ref):
+    total = in_ref[0]
+    for i in range(1, in_ref.shape[0]):
+        total += in_ref[i]
     out_ref[...] = total
-    for i in range(nx):
-        for j in range(2):
-            ask_ref[j, i * tok : (i + 1) * tok] = in_ref[i, rows + j * tok : rows + (j + 1) * tok]
 
 
 def update_kernel(scale, in_ref, w_ref, out_ref):
@@ -136,12 +129,14 @@
     return total
 
 
-def inner_kernel(own_ref, other_ref, ask_ref, w_ref, out_ref, piece_ref, pair_ref, kept_ref, sems):
+def inner_kernel(own_ref, other_ref, w_ref, q_ref, c_ref, out_ref, piece_ref, ask_ref, pair_ref, kept_ref, sems):
     nx, rows, width = w_ref.shape
     units = rows // 3
     n = nx * units
     tok = own_ref.shape[0]
-    copies = start_all([(own_ref, pair_ref.at[:tok]), (other_ref, pair_ref.at[tok:]), (w_ref, kept_ref)], sems)
+    pairs = [(q_ref.at[1], ask_ref.at[:, :width]), (c_ref.at[1], ask_ref.at[:, width:])]
+    pairs += [(own_ref, pair_ref.at[:tok]), (other_ref, pair_ref.at[tok:]), (w_ref, kept_ref)]
+    copies = start_all(pairs, sems)
     piece = piece_ref.shape[0]
     start = pl.multiple_of(lax.axis_index("z") * piece, 8)
     piece_ref[...] = w_ref[lax.axis_index("x"), pl.ds(start, piece)]
@@ -152,38 +147,28 @@
     )
     out_ref[:, :units] = in_sum[:n].reshape(nx, units, width)
     out_ref[:, units : 2 * units] = in_sum[n:].reshape(nx, units, width)
-    out_ref[:, 2 * units : rows] = down_sum.reshape(nx, units, width)
-    for i in range(nx):
-        out_ref[i, rows:] = ask_ref[...]
+    out_ref[:, 2 * units :] = down_sum.reshape(nx, units, width)
     for copy in copies:
         copy.wait()
 
 
-def outer_kernel(ask_ref, got_ref, w_ref, out_ref, pair_ref, sems):
+def outer_kernel(ask_ref, w_hbm_ref, out_ref, w_ref, rows_ref, sems):
+    units = w_ref.shape[0] // 3
     width = w_ref.shape[1]
-    units = w_ref.shape[0] // 3
-    tok = pair_ref.shape[0] // 2
-    at = pl.ds(pl.multiple_of(lax.axis_index("x") * tok, 8), tok)
-    copies = start_all(
-        [
-            (ask_ref.at[0, at], pair_ref.at[:tok, :width]),
-            (ask_ref.at[1, at], pair_ref.at[:tok, width:]),
-            (got_ref.at[0, at], pair_ref.at[tok:, :width]),
-            (got_ref.at[1, at], pair_ref.at[tok:, width:]),
-        ],
-        sems,
-    )
-    step = 256
-    chunks = [
-        (ref[0, at : at + step], ref[1, at : at + step])
-        for ref in (ask_ref, got_ref)
-        for at in range(0, ref.shape[1], step)
-    ]
-    in_sum, down_sum = weight_grad(split(w_ref[: 2 * units]), split(w_ref[2 * units :]), chunks)
-    out_ref[: 2 * units] = in_sum
-    out_ref[2 * units :] = down_sum
-    for copy in copies:
-        copy.wait()
+    n, step = rows_ref.shape[:2]
+    pairs = [(w_hbm_ref, w_ref)] + [(ask_ref.at[i * step : (i + 1) * step], rows_ref.at[i]) for i in range(n)]
+    copies = start_all(pairs, sems)
+    copies.pop(0).wait()
+    w_in, w_down = split(w_ref[: 2 * units]), split(w_ref[2 * units :])
+    for i in range(n):
+        copies[i].wait()
+        in_sum, down_sum = weight_grad(w_in, w_down, [(rows_ref[i, :, :width], rows_ref[i, :, width:])])
+        if i == 0:
+            out_ref[: 2 * units] = in_sum
+            out_ref[2 * units :] = down_sum
+        else:
+            out_ref[: 2 * units] += in_sum
+            out_ref[2 * units :] += down_sum
 
 
 def query_grad(rows, cots, w_gate, w_up, w_down, up_way, down_way):
@@ -196,20 +181,28 @@
     )
 
 
-def query_kernel(q_ref, c_ref, wg_ref, wu_ref, wd_ref, pair_ref, w_ref, zero_ref, mine_ref, theirs_ref):
-    tok, width = zero_ref.shape
-    zero_ref[...] = query_grad(
+def zero_kernel(q_ref, c_ref, wg_ref, wu_ref, wd_ref, out_ref):
+    out_ref[...] = query_grad(
         q_ref[0], c_ref[0], split(wg_ref[0]), split(wu_ref[0]), split(wd_ref[0]), NN, NT
     )
+
+
+def one_kernel(q_ref, c_ref, w_ref, zero_ref, out_ref):
     w_gate, w_up, w_down = [split(w) for w in parts(w_ref, w_ref.shape[1] // 3)]
-    grad = query_grad(pair_ref[:, :width], pair_ref[:, width:], w_gate, w_up, w_down, NT, NN)
-    mine_ref[...] = grad[:tok]
-    theirs_ref[...] = grad[tok:]
-
-
-def final_kernel(d_ref, pair_ref, w_ref, query_ref, mine_ref, theirs_ref):
+    out_ref[0] = zero_ref[...]
+    out_ref[1] = query_grad(q_ref[1], c_ref[1], w_gate, w_up, w_down, NT, NN)
+
+
+def load_kernel(pair_ref, w_ref, pair_out_ref, w_out_ref, sems):
+    for copy in start_all([(pair_ref, pair_out_ref), (w_ref, w_out_ref)], sems):
+        copy.wait()
+
+
+def final_kernel(d_ref, pair_ref, w_ref, new_ref, mine_ref, theirs_ref, new_out_ref, sems):
+    copies = start_all([(new_ref, new_out_ref)], sems)
     width = d_ref.shape[2]
     units = d_ref.shape[1] // 3
+    d_gate, d_up, d_down = [split(d) for d in parts(d_ref, units)]
     w_gate, w_up, w_down = [split(w) for w in parts(w_ref, units)]
     rows, cots = split(pair_ref[:, :width]), split(pair_ref[:, width:])
     gate, up_part = dot3(rows, w_gate, NT), dot3(rows, w_up, NT)
@@ -217,7 +210,6 @@
     sigma, active, slope = gates(gate)
     bend = sigma * (1.0 - sigma) * (2.0 + gate * (1.0 - 2.0 * sigma))
     steep = slope * up_part
-    d_gate, d_up, d_down = [split(d) for d in parts(d_ref, units)]
     d_g, d_u = dot3(rows, d_gate, NT), dot3(rows, d_up, NT)
     d_c = dot3(cots, d_down, NT)
     d_h = steep * d_g + active * d_u
@@ -234,14 +226,12 @@
     mine_ref[:, :width] = key[:tok]
     mine_ref[:, width:] = value[:tok]
     theirs_ref[:, :width] = key[tok:]
-    theirs_ref[:, width : 2 * width] = value[tok:]
-    theirs_ref[:, 2 * width :] = query_ref[...]
-
-
-def join_kernel(scale, mine_ref, got_ref, rate_ref, zero_ref, one_ref, q_ref, k_ref, v_ref):
+    theirs_ref[:, width:] = value[tok:]
+    copies[0].wait()
+
+
+def join_kernel(scale, mine_ref, got_ref, rate_ref, k_ref, v_ref):
     width = k_ref.shape[1]
-    q_ref[0] = zero_ref[...]
-    q_ref[1] = one_ref[...] + got_ref[:, 2 * width :]
     k_ref[...] = scale * (mine_ref[:, :width] + got_ref[:, :width])
     rate = scale * rate_ref[...]
     for at in range(0, width, LANES):
@@ -267,7 +257,6 @@
     scale = float(tok * NX * NC * n_z) ** (-0.5)
     f32 = lambda *shape: jax.ShapeDtypeStruct(shape, jnp.float32)
     swap = lambda x: lax.ppermute(x, "c", [(i, (i + 1) % NC) for i in range(NC)])
-    gather = lambda x: lax.all_gather(x, "x", axis=0, tiled=True)
     exchange = lambda x: lax.all_to_all(x.reshape(n_z, piece, width), "z", 0, 0)
     hold = lambda x: pltpu.with_memory_space_constraint(x, pltpu.HBM)
     n_mul = 2 * tok * width * half
@@ -286,57 +275,78 @@
         ],
     )(hold(keys), hold(values), hold(rates.reshape(1, tok)))
     other = swap(own)
-    w_rows, ask = call(
+    w_rows = call(
         units_kernel,
-        [f32(NX, 3 * units, width), f32(2 * tok, width)],
+        f32(NX, 3 * units, width),
         0,
         2 * n_w,
-        in_specs=[there] * 5,
-        out_specs=[here] * 2,
-        scratch_shapes=[pltpu.VMEM((2, width, half), jnp.float32), pltpu.SemaphoreType.DMA((4 + NX,))],
-    )(hold(w_gate), hold(w_up), hold(w_down), hold(queries), hold(grad_out))
+        in_specs=[there] * 3,
+        out_specs=here,
+        scratch_shapes=[pltpu.VMEM((2, width, half), jnp.float32), pltpu.SemaphoreType.DMA((2 + NX,))],
+    )(hold(after(w_gate, own)), hold(w_up), hold(w_down))
 
     pair_shape = pltpu.HBM((2 * tok, 2 * width), jnp.float32)
     kept_shape = pltpu.HBM((NX, 3 * units, width), jnp.float32)
-    inner, w_piece, pair, kept = call(
+    inner, w_piece, ask, pair, kept = call(
         inner_kernel,
-        [f32(NX, 3 * units + 2 * tok, width), f32(piece, width), pair_shape, kept_shape],
+        [f32(NX, 3 * units, width), f32(piece, width), f32(tok, 2 * width), pair_shape, kept_shape],
         36 * n_mul,
         2 * n_w,
-        in_specs=[here] * 4,
-        out_specs=[here, here, there, there],
-        scratch_shapes=[pltpu.SemaphoreType.DMA((3,))],
-    )(own, other, ask, w_rows)
+        in_specs=[here, here, here, there, there],
+        out_specs=[here, here, here, there, there],
+        scratch_shapes=[pltpu.SemaphoreType.DMA((5,))],
+    )(own, other, w_rows, hold(queries), hold(grad_out))
+    ask = lax.all_gather(ask, ("x", "c"), axis=0, tiled=True)
     inner = lax.all_to_all(inner, "x", 0, 0)
-    inner, ask = call(row_sum_kernel, [f32(3 * units, width), f32(2, NX * tok, width)], 0, 4 * n_w)(inner)
+    inner = call(row_sum_kernel, f32(3 * units, width), 0, 2 * n_w)(inner)
     pieces = f32(n_z, piece, width)
     new = call(functools.partial(update_kernel, scale), pieces, 0, n_w)(exchange(inner), w_piece)
-    ask_got = swap(after(ask, new))
-    new, ask_got = both(exchange(new).reshape(3 * units, width), ask_got)
-
-    outer, asked = call(
+    new = exchange(new).reshape(3 * units, width)
+
+    outer = call(
         outer_kernel,
-        [f32(3 * units, width), pair_shape],
+        f32(3 * units, width),
         36 * n_mul,
         64 * tok * width,
-        in_specs=[here] * 3,
-        out_specs=[here, there],
-        scratch_shapes=[pltpu.SemaphoreType.DMA((4,))],
-    )(ask, ask_got, new)
-    got, new_x = both(exchange(outer), gather(after(new, outer)))
-    outer = call(total_kernel, pieces, 0, n_w)(got)
-    new_x = after(new_x, outer).reshape(NX, 3 * units, width)
-    zero, one, one_theirs = call(query_kernel, [f32(tok, width)] * 3, 60 * n_mul, 4 * n_w)(
-        queries, grad_out, w_gate, w_up, w_down, asked, new_x
-    )
-    outer, one_theirs = both(exchange(outer).reshape(3 * units, width), one_theirs)
-    d_all = gather(outer).reshape(NX, 3 * units, width)
-    mine, theirs = call(
-        final_kernel, [f32(tok, 2 * width), f32(tok, 3 * width)], 72 * n_mul, 3 * n_w
-    )(d_all, pair, kept, one_theirs)
-    return call(
-        functools.partial(join_kernel, scale), [f32(2, tok, width), f32(tok, width), f32(tok, width)], 0, 40 * tok * width
-    )(mine, swap(theirs), rate, zero, one)
+        in_specs=[there, there],
+        out_specs=here,
+        scratch_shapes=[
+            pltpu.VMEM((3 * units, width), jnp.float32),
+            pltpu.VMEM((4, NX * NC * tok // 4, 2 * width), jnp.float32),
+            pltpu.SemaphoreType.DMA((5,)),
+        ],
+    )(hold(ask), hold(new))
+    new_all = lax.all_gather(new, ("x", "c"), axis=0, tiled=False)
+    outer = call(total_kernel, pieces, 0, n_w)(exchange(outer))
+    zero = call(zero_kernel, f32(tok, width), 30 * n_mul, 2 * n_w)(
+        after(queries, outer), grad_out, w_gate, w_up, w_down
+    )
+    loaded = call(
+        load_kernel,
+        [f32(2 * tok, 2 * width), f32(NX, 3 * units, width)],
+        0,
+        4 * n_w,
+        in_specs=[there] * 2,
+        out_specs=[here] * 2,
+        scratch_shapes=[pltpu.SemaphoreType.DMA((2,))],
+    )(hold(after(pair, zero)), hold(kept))
+    outer, loaded = both(exchange(outer).reshape(3 * units, width), loaded)
+    d_all, new_all = both(lax.all_gather(outer, "x", axis=0, tiled=False), new_all)
+    mine, theirs, new_all = call(
+        final_kernel,
+        [f32(tok, 2 * width)] * 2 + [f32(*new_all.shape)],
+        72 * n_mul,
+        3 * n_w,
+        in_specs=[here, here, here, there],
+        out_specs=[here] * 3,
+        scratch_shapes=[pltpu.SemaphoreType.DMA((1,))],
+    )(d_all, *loaded, hold(new_all))
+    grad_queries = call(one_kernel, f32(2, tok, width), 30 * n_mul, 2 * n_w)(queries, grad_out, new_all, zero)
+    theirs, grad_queries = both(swap(theirs), grad_queries)
+    grad_keys, grad_values = call(
+        functools.partial(join_kernel, scale), [f32(tok, width)] * 2, 0, 24 * tok * width
+    )(mine, theirs, rate)
+    return grad_queries, grad_keys, grad_values
 
 
 def solution(mesh):

time: 150 us -> 140 us (0.933)
  starting transfers between devices: 39.9 us -> 26 us
  between operations: 0.81 us -> 14.2 us
  blocking collectives: 84.1 us -> 74.3 us
  Pallas kernels: 11.1 us -> 15.4 us
  local copies, waits for them, and re-layouts: 3.23 us -> 0.03 us
    all_to_all x2 -> x3, blocking collectives: 34.3 us -> 48.6 us  [body(): exchange = lambda x: lax.all_to_all(x.reshape(n_z, piece, width), 'z', 0, 0)]
    all_gather x2 -> x1, blocking collectives: 24.1 us -> 11.3 us  [body(): lax.all_gather(outer, 'x', axis=0, tiled=False)]
    all_to_all x1, blocking collectives: 25.7 us -> 14.5 us  [body(): inner = lax.all_to_all(inner, 'x', 0, 0)]
    all_to_all x2 -> x1, starting transfers between devices: 12.7 us -> 3.53 us  [body(): exchange = lambda x: lax.all_to_all(x.reshape(n_z, piece, width), 'z', 0, 0)]
    ppermute x3 -> x2, starting transfers between devices: 27.2 us -> 22.4 us  [body(): lax.ppermute(x, 'c', [(i, (i + 1) % NC) for i in range(NC)])]
    pallas_call x8 -> x10, Pallas kernels: 10.1 us -> 14.3 us  [the longest x1 3.14 us: body(): call(outer_kernel, f32(3 * units, width), 36 * n_mul, 64 * tok * width, i...]
    unnamed x16 -> x10, local copies, waits for them, and re-layouts: 3.23 us -> 0.03 us
    all_to_all x2 -> x1, waiting for transfers between devices: 8.47 us -> 9.37 us  [body(): exchange = lambda x: lax.all_to_all(x.reshape(n_z, piece, width), 'z', 0, 0)]
  transfers between devices with their start and end apart: 5 -> 5, of which waited for: 2 -> 1; matrix products, arithmetic and copies ran while one was open for 0% -> 0% of each run, Pallas kernels for 2% -> 7%
where the time goes in v2:
time: 140 us; the launch traced here: 139 us
  blocking collectives  74.3 us (53%)
  starting transfers between devices  26 us (19%)
  Pallas kernels  15.4 us (11%)
  between operations  14.2 us (10%)
  waiting for transfers between devices  9.43 us (7%)
    all_to_all x3, blocking collectives, body(): exchange = lambda x: lax.all_to_all(x.reshape(n_z, piece, width), 'z', 0, 0)  48.6 us
    ppermute x2, starting transfers between devices, body(): lax.ppermute(x, 'c', [(i, (i + 1) % NC) for i in range(NC)])  22.4 us
    all_to_all x1, blocking collectives, body(): inner = lax.all_to_all(inner, 'x', 0, 0)  14.5 us
    all_gather x1, blocking collectives, body(): lax.all_gather(outer, 'x', axis=0, tiled=False)  11.3 us
    all_to_all x1, waiting for transfers between devices, body(): exchange = lambda x: lax.all_to_all(x.reshape(n_z, piece, width), 'z', 0, 0)  9.37 us
    all_to_all x1, starting transfers between devices, body(): exchange = lambda x: lax.all_to_all(x.reshape(n_z, piece, width), 'z', 0, 0)  3.53 us
    pallas_call x1, Pallas kernels, body(): call(outer_kernel, f32(3 * units, width), 36 * n_mul, 64 * tok * width, i...  3.14 us
  transfers between devices with their start and end apart: 5, of which 1 were waited for; matrix products, arithmetic and copies ran while one was open for 0% of the time, Pallas kernels for 7%

profile of v2, /device:TPU:1, one launch (start us, length us, event | category | flops | bytes accessed | tf_op | source)
XLA Modules:
  0.0 139.3 jit_solution(16243546668185952693)
XLA Ops:
  7.2 0.0 all-gather.4.cloned.1.call-start
  7.2 1.0 shard_map.103
  8.2 12.4 %collective-permute-start = (f32[128,512]{1,0:T(8,128)S(1)}, f32[128,512]{1,0:T(8,128)S(1)}, u32[]{:S(2)}, u32[]{:S(2)}) collective-permute-start(f32[128,512]{1,0:T(8,128)S(1)} %get-tuple-element.27.own_ref), channel_id=1, source_target_pairs={{0,8},{8,0},{1,9},{9,1},{2,10},{10,2},{3,11},{11,3},{4,12},{12,4},... | collective-permute-start | bytes 786440 | tf_op jit(solution)/shard_map/ppermute | solution.py:259
  20.7 1.3 shard_map.104.w_ref
  22.0 0.0 collective-permute-done.other_ref
  22.0 2.0 %shard_map.105 = (f32[4,192,256]{2,1,0:T(8,128)S(1)}, f32[16,256]{1,0:T(8,128)S(1)}, f32[128,512]{1,0:T(8,128)}, f32[256,512]{1,0:T(8,128)}, f32[4,192,256]{2,1,0:T(8,128)}) custom-call(f32[128,512]{1,0:T(8,128)S(1)} %get-tuple-element.27.own_ref, f32[128,512]{1,0:T(8,128)S(1)} %collective-permute-done.other_ref, f32[4,192,256]{2,1,0:T(8,128)S(1)} %shard_map.104.w_ref, ...), custom_call_target="tpu_custom_call" | custom-call | flops 603979776 | bytes 1572864 | tf_op jit(solution)/shard_map/pallas_call | solution.py:290
  24.0 0.0 all-gather.4.cloned.1.call-update
  24.0 0.0 all-gather.6.cloned.1.call-start
  24.1 14.5 %all_to_all.25.in_ref = f32[4,192,256]{2,1,0:T(8,128)S(1)} all-to-all(f32[4,192,256]{2,1,0:T(8,128)S(1)} %get-tuple-element.30), channel_id=1, replica_groups=mesh['z'=12,'x'=4,'c'=2,'head'=8] {'x'}, dimensions={0} | all-to-all | bytes 1572864 | tf_op jit(solution)/shard_map/all_to_all | solution.py:300
  38.6 18.5 %all_to_all.26.in_ref = f32[12,16,256]{2,1,0:T(8,128)S(1)} all-to-all(f32[12,16,256]{2,1,0:T(8,128)S(1)} %bitcast.9), channel_id=1, replica_groups=mesh['z'=12,'x'=4,'c'=2,'head'=8] {'z'}, dimensions={0} | all-to-all | bytes 393216 | tf_op jit(solution)/shard_map/all_to_all | solution.py:260
  57.1 15.3 %all_to_all.27 = f32[12,16,256]{2,1,0:T(8,128)} all-to-all(f32[12,16,256]{2,1,0:T(8,128)S(1)} %shard_map.107), channel_id=1, replica_groups=mesh['z'=12,'x'=4,'c'=2,'head'=8] {'z'}, dimensions={0} | all-to-all | bytes 393216 | tf_op jit(solution)/shard_map/all_to_all | solution.py:260
  72.4 0.0 all-gather.6.cloned.1.call-update
  72.4 0.0 all-gather.4.cloned.1.call-done.ask_ref
  72.5 0.0 copy-start
  72.5 0.0 copy-start.1
  72.5 0.0 copy-start.2
  72.5 0.0 copy-start.3
  72.5 0.0 copy-start.4
  72.5 3.1 %shard_map.108 = f32[192,256]{1,0:T(8,128)S(1)} custom-call(f32[1024,512]{1,0:T(8,128)} %all-gather.4.cloned.1.call-done.ask_ref, f32[192,256]{1,0:T(8,128)} %bitcast.11), custom_call_target="tpu_custom_call" | custom-call | flops 603979776 | bytes 2097152 | tf_op jit(solution)/shard_map/pallas_call | solution.py:306
  75.7 14.8 %all_to_all.28.in_ref = f32[12,16,256]{2,1,0:T(8,128)S(1)} all-to-all(f32[12,16,256]{2,1,0:T(8,128)S(1)} %bitcast.7), channel_id=1, replica_groups=mesh['z'=12,'x'=4,'c'=2,'head'=8] {'z'}, dimensions={0} | all-to-all | bytes 393216 | tf_op jit(solution)/shard_map/all_to_all | solution.py:260
  90.4 0.7 shard_map.109
  91.1 3.5 %all-to-all-start.4 = ((f32[12,16,256]{2,1,0:T(8,128)}), f32[12,16,256]{2,1,0:T(8,128)S(1)}, u32[]{:S(2)}, u32[]{:S(2)}) async-start(f32[12,16,256]{2,1,0:T(8,128)} %shard_map.109), calls=%async_computation.4 | async-start | bytes 393216 | tf_op jit(solution)/shard_map/all_to_all | solution.py:260
  94.7 0.0 copy-done
  94.7 0.0 copy-done.1
  94.7 0.0 copy-done.2
  94.7 0.0 copy-done.3
  94.7 0.0 copy-done.4
  94.7 1.3 shard_map.110.zero_ref
  96.1 1.3 shard_map.111
  97.4 9.4 %all-to-all-done.4 = f32[12,16,256]{2,1,0:T(8,128)S(1)} async-done(((f32[12,16,256]{2,1,0:T(8,128)}), f32[12,16,256]{2,1,0:T(8,128)S(1)}, u32[]{:S(2)}, u32[]{:S(2)}) %all-to-all-start.4) | async-done | bytes 196640 | tf_op jit(solution)/shard_map/all_to_all | solution.py:260
  106.7 11.3 %all-gather = f32[768,256]{1,0:T(8,128)S(1)} all-gather(f32[192,256]{1,0:T(8,128)S(1)} %bitcast.12), channel_id=2, replica_groups=mesh['z'=12,'x'=4,'c'=2,'head'=8] {'x'}, dimensions={0}, use_global_device_ids=true | all-gather | bytes 983040 | tf_op jit(solution)/shard_map/all_gather | solution.py:334
  118.0 0.0 all-gather.6.cloned.1.call-done.new_ref
  118.0 1.8 %shard_map.112 = (f32[128,512]{1,0:T(8,128)S(1)}, f32[128,512]{1,0:T(8,128)S(1)}, f32[8,192,256]{2,1,0:T(8,128)S(1)}) custom-call(f32[4,192,256]{2,1,0:T(8,128)S(1)} %bitcast.8, f32[256,512]{1,0:T(8,128)S(1)} %get-tuple-element.40.pair_ref, f32[4,192,256]{2,1,0:T(8,128)S(1)} %get-tuple-element.41.w_ref, f32[8,192,256]{2,1,0:T(8,128)} %all-gather.6.cloned.1.call-done.new_ref), custom_call_target="tpu_custom_call" | custom-call | flops 1207959552 | bytes 2359296 | tf_op jit(solution)/shard_map/pallas_call | solution.py:335
  119.8 9.9 %collective-permute-start.1 = (f32[128,512]{1,0:T(8,128)S(1)}, f32[128,512]{1,0:T(8,128)S(1)}, u32[]{:S(2)}, u32[]{:S(2)}) collective-permute-start(f32[128,512]{1,0:T(8,128)S(1)} %get-tuple-element.43), channel_id=1, source_target_pairs={{0,8},{8,0},{1,9},{9,1},{2,10},{10,2},{3,11},{11,3},{4,12},{12,4},... | collective-permute-start | bytes 786440 | tf_op jit(solution)/shard_map/ppermute | solution.py:259
  129.8 1.9 %shard_map.113 = f32[2,128,256]{2,1,0:T(8,128)} custom-call(f32[2,128,256]{2,1,0:T(8,128)S(1)} %copy-done.3, f32[2,128,256]{2,1,0:T(8,128)S(1)} %copy-done.4, f32[8,192,256]{2,1,0:T(8,128)S(1)} %get-tuple-element.44.w_ref, f32[128,256]{1,0:T(8,128)S(1)} %shard_map.110.zero_ref), custom_call_target="tpu_custom_call" | custom-call | flops 503316480 | bytes 1572864 | tf_op jit(solution)/shard_map/pallas_call | solution.py:344
  131.7 0.0 collective-permute-done.1.got_ref
  131.7 0.7 shard_map.114
  (2 shorter events, 0.1 us)
Async XLA Ops:
  7.2 65.3 %all-gather.4.cloned.1.call-start = ((), (), s32[]{:S(2)}) async-start(), calls=%async_computation.5 | async-start | bytes 2359296 | tf_op jit(solution)/shard_map/all_gather | solution.py:299
  8.2 13.7 %collective-permute-start = (f32[128,512]{1,0:T(8,128)S(1)}, f32[128,512]{1,0:T(8,128)S(1)}, u32[]{:S(2)}, u32[]{:S(2)}) collective-permute-start(f32[128,512]{1,0:T(8,128)S(1)} %get-tuple-element.27.own_ref), channel_id=1, source_target_pairs={{0,8},{8,0},{1,9},{9,1},{2,10},{10,2},{3,11},{11,3},{4,12},{12,4},... | collective-permute-start | bytes 786440 | tf_op jit(solution)/shard_map/ppermute | solution.py:259
  24.0 94.0 %all-gather.6.cloned.1.call-start = ((), (), s32[]{:S(2)}) async-start(), calls=%async_computation.6 | async-start | bytes 1769472 | tf_op jit(solution)/shard_map/all_gather | solution.py:319
  72.5 22.2 %copy-start = (f32[1,256,512]{2,1,0:T(8,128)S(1)}, f32[1,256,512]{2,1,0:T(8,128)}, u32[]{:S(2)}) copy-start(f32[1,256,512]{2,1,0:T(8,128)} %wg_ref.2) | copy-start | bytes 1572868
  72.5 22.2 %copy-start.1 = (f32[1,256,512]{2,1,0:T(8,128)S(1)}, f32[1,256,512]{2,1,0:T(8,128)}, u32[]{:S(2)}) copy-start(f32[1,256,512]{2,1,0:T(8,128)} %wu_ref.3) | copy-start | bytes 1572868
  72.5 22.2 %copy-start.2 = (f32[1,512,256]{2,1,0:T(8,128)S(1)}, f32[1,512,256]{2,1,0:T(8,128)}, u32[]{:S(2)}) copy-start(f32[1,512,256]{2,1,0:T(8,128)} %wd_ref.3) | copy-start | bytes 1572868
  72.5 22.2 %copy-start.3 = (f32[2,128,256]{2,1,0:T(8,128)S(1)}, f32[2,128,256]{2,1,0:T(8,128)}, u32[]{:S(2)}) copy-start(f32[2,128,256]{2,1,0:T(8,128)} %q_ref.4) | copy-start | bytes 786436
  72.5 22.2 %copy-start.4 = (f32[2,128,256]{2,1,0:T(8,128)S(1)}, f32[2,128,256]{2,1,0:T(8,128)}, u32[]{:S(2)}) copy-start(f32[2,128,256]{2,1,0:T(8,128)} %c_ref.5) | copy-start | bytes 786436
  91.1 15.6 %all-to-all-start.4 = ((f32[12,16,256]{2,1,0:T(8,128)}), f32[12,16,256]{2,1,0:T(8,128)S(1)}, u32[]{:S(2)}, u32[]{:S(2)}) async-start(f32[12,16,256]{2,1,0:T(8,128)} %shard_map.109), calls=%async_computation.4 | async-start | bytes 393216 | tf_op jit(solution)/shard_map/all_to_all | solution.py:260
  119.8 11.9 %collective-permute-start.1 = (f32[128,512]{1,0:T(8,128)S(1)}, f32[128,512]{1,0:T(8,128)S(1)}, u32[]{:S(2)}, u32[]{:S(2)}) collective-permute-start(f32[128,512]{1,0:T(8,128)S(1)} %get-tuple-element.43), channel_id=1, source_target_pairs={{0,8},{8,0},{1,9},{9,1},{2,10},{10,2},{3,11},{11,3},{4,12},{12,4},... | collective-permute-start | bytes 786440 | tf_op jit(solution)/shard_map/ppermute | solution.py:259
Sparse Core Ops, SparseCore 0:
  24.1 30.8 all-gather.3
  72.5 29.1 all-gather.5

commit v3 on v2

--- a/solution.py
+++ b/solution.py
@@ -152,23 +152,19 @@
         copy.wait()
 
 
-def outer_kernel(ask_ref, w_hbm_ref, out_ref, w_ref, rows_ref, sems):
+def outer_kernel(rows_ref, w_ref, out_ref, new_ref, sems):
+    copies = start_all([(w_ref, new_ref)], sems)
+    width = w_ref.shape[1]
     units = w_ref.shape[0] // 3
-    width = w_ref.shape[1]
-    n, step = rows_ref.shape[:2]
-    pairs = [(w_hbm_ref, w_ref)] + [(ask_ref.at[i * step : (i + 1) * step], rows_ref.at[i]) for i in range(n)]
-    copies = start_all(pairs, sems)
-    copies.pop(0).wait()
-    w_in, w_down = split(w_ref[: 2 * units]), split(w_ref[2 * units :])
-    for i in range(n):
-        copies[i].wait()
-        in_sum, down_sum = weight_grad(w_in, w_down, [(rows_ref[i, :, :width], rows_ref[i, :, width:])])
-        if i == 0:
-            out_ref[: 2 * units] = in_sum
-            out_ref[2 * units :] = down_sum
-        else:
-            out_ref[: 2 * units] += in_sum
-            out_ref[2 * units :] += down_sum
+    step = 256
+    chunks = [
+        (rows_ref[at : at + step, :width], rows_ref[at : at + step, width:])
+        for at in range(0, rows_ref.shape[0], step)
+    ]
+    in_sum, down_sum = weight_grad(split(w_ref[: 2 * units]), split(w_ref[2 * units :]), chunks)
+    out_ref[: 2 * units] = in_sum
+    out_ref[2 * units :] = down_sum
+    copies[0].wait()
 
 
 def query_grad(rows, cots, w_gate, w_up, w_down, up_way, down_way):
@@ -181,25 +177,34 @@
     )
 
 
-def zero_kernel(q_ref, c_ref, wg_ref, wu_ref, wd_ref, out_ref):
+def zero_kernel(q_hbm_ref, c_hbm_ref, wg_hbm_ref, wu_hbm_ref, wd_hbm_ref, out_ref, *refs):
+    *refs, sems = refs
+    pairs = [(ref.at[0], to) for ref, to in zip((q_hbm_ref, c_hbm_ref, wg_hbm_ref, wu_hbm_ref, wd_hbm_ref), refs)]
+    for copy in start_all(pairs, sems):
+        copy.wait()
+    q_ref, c_ref, wg_ref, wu_ref, wd_ref = refs
     out_ref[...] = query_grad(
-        q_ref[0], c_ref[0], split(wg_ref[0]), split(wu_ref[0]), split(wd_ref[0]), NN, NT
+        q_ref[...], c_ref[...], split(wg_ref[...]), split(wu_ref[...]), split(wd_ref[...]), NN, NT
     )
 
 
 def one_kernel(q_ref, c_ref, w_ref, zero_ref, out_ref):
     w_gate, w_up, w_down = [split(w) for w in parts(w_ref, w_ref.shape[1] // 3)]
     out_ref[0] = zero_ref[...]
-    out_ref[1] = query_grad(q_ref[1], c_ref[1], w_gate, w_up, w_down, NT, NN)
-
-
-def load_kernel(pair_ref, w_ref, pair_out_ref, w_out_ref, sems):
-    for copy in start_all([(pair_ref, pair_out_ref), (w_ref, w_out_ref)], sems):
-        copy.wait()
-
-
-def final_kernel(d_ref, pair_ref, w_ref, new_ref, mine_ref, theirs_ref, new_out_ref, sems):
-    copies = start_all([(new_ref, new_out_ref)], sems)
+    out_ref[1] = query_grad(q_ref[...], c_ref[...], w_gate, w_up, w_down, NT, NN)
+
+
+def load_kernel(*refs):
+    *refs, sems = refs
+    n = len(refs) // 2
+    for copy in start_all(list(zip(refs[:n], refs[n:])), sems):
+        copy.wait()
+
+
+def final_kernel(
+    d_ref, pair_ref, w_ref, new_ref, q_ref, c_ref, mine_ref, theirs_ref, new_out_ref, q_out_ref, c_out_ref, sems
+):
+    copies = start_all([(new_ref, new_out_ref), (q_ref.at[1], q_out_ref), (c_ref.at[1], c_out_ref)], sems)
     width = d_ref.shape[2]
     units = d_ref.shape[1] // 3
     d_gate, d_up, d_down = [split(d) for d in parts(d_ref, units)]
@@ -227,7 +232,8 @@
     mine_ref[:, width:] = value[:tok]
     theirs_ref[:, :width] = key[tok:]
     theirs_ref[:, width:] = value[tok:]
-    copies[0].wait()
+    for copy in copies:
+        copy.wait()
 
 
 def join_kernel(scale, mine_ref, got_ref, rate_ref, k_ref, v_ref):
@@ -301,47 +307,56 @@
     inner = call(row_sum_kernel, f32(3 * units, width), 0, 2 * n_w)(inner)
     pieces = f32(n_z, piece, width)
     new = call(functools.partial(update_kernel, scale), pieces, 0, n_w)(exchange(inner), w_piece)
-    new = exchange(new).reshape(3 * units, width)
-
-    outer = call(
+    load = lambda *args: call(
+        load_kernel,
+        [f32(*a.shape) for a in args],
+        0,
+        8 * sum(a.size for a in args),
+        in_specs=[there] * len(args),
+        out_specs=[here] * len(args),
+        scratch_shapes=[pltpu.SemaphoreType.DMA((len(args),))],
+    )(*[hold(a) for a in args])
+    (ask,) = load(after(ask, new))
+    new, ask = both(exchange(new).reshape(3 * units, width), ask)
+
+    outer, new = call(
         outer_kernel,
-        f32(3 * units, width),
+        [f32(3 * units, width), pltpu.HBM((3 * units, width), jnp.float32)],
         36 * n_mul,
         64 * tok * width,
-        in_specs=[there, there],
+        in_specs=[here, here],
+        out_specs=[here, there],
+        scratch_shapes=[pltpu.SemaphoreType.DMA((1,))],
+    )(ask, new)
+    new_all = lax.all_gather(new, ("x", "c"), axis=0, tiled=False)
+    outer = call(total_kernel, pieces, 0, n_w)(exchange(outer))
+    vmem = lambda *shape: pltpu.VMEM(shape, jnp.float32)
+    zero = call(
+        zero_kernel,
+        f32(tok, width),
+        30 * n_mul,
+        2 * n_w,
+        in_specs=[there] * 5,
         out_specs=here,
         scratch_shapes=[
-            pltpu.VMEM((3 * units, width), jnp.float32),
-            pltpu.VMEM((4, NX * NC * tok // 4, 2 * width), jnp.float32),
+            vmem(tok, width), vmem(tok, width), vmem(width, hidden), vmem(width, hidden), vmem(hidden, width),
             pltpu.SemaphoreType.DMA((5,)),
         ],
-    )(hold(ask), hold(new))
-    new_all = lax.all_gather(new, ("x", "c"), axis=0, tiled=False)
-    outer = call(total_kernel, pieces, 0, n_w)(exchange(outer))
-    zero = call(zero_kernel, f32(tok, width), 30 * n_mul, 2 * n_w)(
-        after(queries, outer), grad_out, w_gate, w_up, w_down
-    )
-    loaded = call(
-        load_kernel,
-        [f32(2 * tok, 2 * width), f32(NX, 3 * units, width)],
-        0,
-        4 * n_w,
-        in_specs=[there] * 2,
-        out_specs=[here] * 2,
-        scratch_shapes=[pltpu.SemaphoreType.DMA((2,))],
-    )(hold(after(pair, zero)), hold(kept))
+    )(*[hold(a) for a in (after(queries, outer), grad_out, w_gate, w_up, w_down)])
+    loaded = load(after(pair, zero), kept)
     outer, loaded = both(exchange(outer).reshape(3 * units, width), loaded)
     d_all, new_all = both(lax.all_gather(outer, "x", axis=0, tiled=False), new_all)
-    mine, theirs, new_all = call(
+    mine, theirs, *ones = call(
         final_kernel,
-        [f32(tok, 2 * width)] * 2 + [f32(*new_all.shape)],
+        [f32(tok, 2 * width)] * 2 + [f32(*new_all.shape), f32(tok, width), f32(tok, width)],
         72 * n_mul,
         3 * n_w,
-        in_specs=[here, here, here, there],
-        out_specs=[here] * 3,
-        scratch_shapes=[pltpu.SemaphoreType.DMA((1,))],
-    )(d_all, *loaded, hold(new_all))
-    grad_queries = call(one_kernel, f32(2, tok, width), 30 * n_mul, 2 * n_w)(queries, grad_out, new_all, zero)
+        in_specs=[here, here, here, there, there, there],
+        out_specs=[here] * 5,
+        scratch_shapes=[pltpu.SemaphoreType.DMA((3,))],
+    )(d_all, *loaded, *[hold(a) for a in (new_all, queries, grad_out)])
+    new_all, q_one, c_one = ones
+    grad_queries = call(one_kernel, f32(2, tok, width), 30 * n_mul, 2 * n_w)(q_one, c_one, new_all, zero)
     theirs, grad_queries = both(swap(theirs), grad_queries)
     grad_keys, grad_values = call(
         functools.partial(join_kernel, scale), [f32(tok, width)] * 2, 0, 24 * tok * width

time: 140 us -> 139 us (level)
  blocking collectives: 74.3 us -> 59.4 us
  waiting for transfers between devices: 9.43 us -> 17.2 us
  starting transfers between devices: 26 us -> 30 us
  Pallas kernels: 15.4 us -> 17.9 us
    all_to_all x3 -> x2, blocking collectives: 48.6 us -> 33.5 us  [body(): exchange = lambda x: lax.all_to_all(x.reshape(n_z, piece, width), 'z', 0, 0)]
    all_to_all x1 -> x2, waiting for transfers between devices: 9.37 us -> 17.2 us  [body(): exchange = lambda x: lax.all_to_all(x.reshape(n_z, piece, width), 'z', 0, 0)]
    all_to_all x1 -> x2, starting transfers between devices: 3.53 us -> 7.86 us  [body(): exchange = lambda x: lax.all_to_all(x.reshape(n_z, piece, width), 'z', 0, 0)]
    pallas_call x4 -> x5, Pallas kernels: 7.61 us -> 9.45 us  [the longest x2 2.97 us: body(): call(load_kernel, [f32(*a.shape) for a in args], 0, 8 * sum((a.size for a...]
  transfers between devices with their start and end apart: 5 -> 6, of which waited for: 1 -> 2; matrix products, arithmetic and copies ran while one was open for 0% -> 0% of each run, Pallas kernels for 7% -> 8%
where the time goes in v3:
time: 139 us
  blocking collectives  59.4 us (43%)
  starting transfers between devices  30 us (22%)
  Pallas kernels  17.9 us (13%)
  waiting for transfers between devices  17.2 us (12%)
  between operations  14.2 us (10%)
    all_to_all x2, blocking collectives, body(): exchange = lambda x: lax.all_to_all(x.reshape(n_z, piece, width), 'z', 0, 0)  33.5 us
    ppermute x2, starting transfers between devices, body(): lax.ppermute(x, 'c', [(i, (i + 1) % NC) for i in range(NC)])  22.1 us
    all_to_all x2, waiting for transfers between devices, body(): exchange = lambda x: lax.all_to_all(x.reshape(n_z, piece, width), 'z', 0, 0)  17.2 us
    all_to_all x1, blocking collectives, body(): inner = lax.all_to_all(inner, 'x', 0, 0)  14.5 us
    all_gather x1, blocking collectives, body(): lax.all_gather(outer, 'x', axis=0, tiled=False)  11.5 us
    all_to_all x2, starting transfers between devices, body(): exchange = lambda x: lax.all_to_all(x.reshape(n_z, piece, width), 'z', 0, 0)  7.86 us
    pallas_call x2, Pallas kernels, body(): call(load_kernel, [f32(*a.shape) for a in args], 0, 8 * sum((a.size for a...  2.97 us
    pallas_call x1, Pallas kernels, body(): call(zero_kernel, f32(tok, width), 30 * n_mul, 2 * n_w, in_specs=[there]...  2.91 us
  transfers between devices with their start and end apart: 6, of which 2 were waited for; matrix products, arithmetic and copies ran while one was open for 0% of the time, Pallas kernels for 8%

profile of v3, /device:TPU:1, one launch (start us, length us, event | category | flops | bytes accessed | tf_op | source)
XLA Modules:
  0.0 138.7 jit_solution(5518744697090886770)
XLA Ops:
  7.2 0.0 all-gather.5.cloned.1.call-start
  7.2 1.0 shard_map.103
  8.2 12.4 %collective-permute-start = (f32[128,512]{1,0:T(8,128)S(1)}, f32[128,512]{1,0:T(8,128)S(1)}, u32[]{:S(2)}, u32[]{:S(2)}) collective-permute-start(f32[128,512]{1,0:T(8,128)S(1)} %get-tuple-element.34.own_ref), channel_id=1, source_target_pairs={{0,8},{8,0},{1,9},{9,1},{2,10},{10,2},{3,11},{11,3},{4,12},{12,4},... | collective-permute-start | bytes 786440 | tf_op jit(solution)/shard_map/ppermute | solution.py:265
  20.7 1.3 shard_map.104.w_ref
  22.0 0.0 collective-permute-done.other_ref
  22.0 2.0 %shard_map.105 = (f32[4,192,256]{2,1,0:T(8,128)S(1)}, f32[16,256]{1,0:T(8,128)S(1)}, f32[128,512]{1,0:T(8,128)}, f32[256,512]{1,0:T(8,128)}, f32[4,192,256]{2,1,0:T(8,128)}) custom-call(f32[128,512]{1,0:T(8,128)S(1)} %get-tuple-element.34.own_ref, f32[128,512]{1,0:T(8,128)S(1)} %collective-permute-done.other_ref, f32[4,192,256]{2,1,0:T(8,128)S(1)} %shard_map.104.w_ref, ...), custom_call_target="tpu_custom_call" | custom-call | flops 603979776 | bytes 1572864 | tf_op jit(solution)/shard_map/pallas_call | solution.py:296
  24.0 0.0 all-gather.5.cloned.1.call-update
  24.0 14.5 %all_to_all.25.in_ref = f32[4,192,256]{2,1,0:T(8,128)S(1)} all-to-all(f32[4,192,256]{2,1,0:T(8,128)S(1)} %get-tuple-element.36), channel_id=1, replica_groups=mesh['z'=12,'x'=4,'c'=2,'head'=8] {'x'}, dimensions={0} | all-to-all | bytes 1572864 | tf_op jit(solution)/shard_map/all_to_all | solution.py:306
  38.5 18.5 %all_to_all.26.in_ref = f32[12,16,256]{2,1,0:T(8,128)S(1)} all-to-all(f32[12,16,256]{2,1,0:T(8,128)S(1)} %bitcast.9), channel_id=1, replica_groups=mesh['z'=12,'x'=4,'c'=2,'head'=8] {'z'}, dimensions={0} | all-to-all | bytes 393216 | tf_op jit(solution)/shard_map/all_to_all | solution.py:266
  57.0 0.7 shard_map.107
  57.7 4.3 %all-to-all-start.2 = ((f32[12,16,256]{2,1,0:T(8,128)}), f32[12,16,256]{2,1,0:T(8,128)S(1)}, u32[]{:S(2)}, u32[]{:S(2)}) async-start(f32[12,16,256]{2,1,0:T(8,128)} %shard_map.107), calls=%async_computation.2 | async-start | bytes 393216 | tf_op jit(solution)/shard_map/all_to_all | solution.py:266
  62.1 0.0 all-gather.7.cloned.1.call-start
  62.1 0.0 all-gather.5.cloned.1.call-done.refs_0_
  62.1 1.6 %shard_map.108.rows_ref = f32[1024,512]{1,0:T(8,128)S(1)} custom-call(f32[1024,512]{1,0:T(8,128)} %all-gather.5.cloned.1.call-done.refs_0_), custom_call_target="tpu_custom_call" | custom-call | bytes 4194304 | tf_op jit(solution)/shard_map/pallas_call | solution.py:310
  63.7 9.4 %all-to-all-done.2 = f32[12,16,256]{2,1,0:T(8,128)S(1)} async-done(((f32[12,16,256]{2,1,0:T(8,128)}), f32[12,16,256]{2,1,0:T(8,128)S(1)}, u32[]{:S(2)}, u32[]{:S(2)}) %all-to-all-start.2) | async-done | bytes 196640 | tf_op jit(solution)/shard_map/all_to_all | solution.py:266
  73.1 1.6 %shard_map.109 = (f32[192,256]{1,0:T(8,128)S(1)}, f32[192,256]{1,0:T(8,128)}) custom-call(f32[1024,512]{1,0:T(8,128)S(1)} %shard_map.108.rows_ref, f32[192,256]{1,0:T(8,128)S(1)} %bitcast.7), custom_call_target="tpu_custom_call" | custom-call | flops 603979776 | bytes 2097152 | tf_op jit(solution)/shard_map/pallas_call | solution.py:322
  74.8 0.0 all-gather.7.cloned.1.call-update
  74.8 14.9 %all_to_all.27.in_ref = f32[12,16,256]{2,1,0:T(8,128)S(1)} all-to-all(f32[12,16,256]{2,1,0:T(8,128)S(1)} %bitcast.10), channel_id=1, replica_groups=mesh['z'=12,'x'=4,'c'=2,'head'=8] {'z'}, dimensions={0} | all-to-all | bytes 393216 | tf_op jit(solution)/shard_map/all_to_all | solution.py:266
  89.7 0.7 shard_map.110
  90.4 3.5 %all-to-all-start.4 = ((f32[12,16,256]{2,1,0:T(8,128)}), f32[12,16,256]{2,1,0:T(8,128)S(1)}, u32[]{:S(2)}, u32[]{:S(2)}) async-start(f32[12,16,256]{2,1,0:T(8,128)} %shard_map.110), calls=%async_computation.4 | async-start | bytes 393216 | tf_op jit(solution)/shard_map/all_to_all | solution.py:266
  94.0 2.9 %shard_map.111.zero_ref = f32[128,256]{1,0:T(8,128)S(1)} custom-call(f32[2,128,256]{2,1,0:T(8,128)} %q_ref.3, f32[2,128,256]{2,1,0:T(8,128)} %c_ref.3, f32[1,256,512]{2,1,0:T(8,128)} %wg_hbm_ref.1, f32[1,256,512]{2,1,0:T(8,128)} %wu_hbm_ref.1, f32[1,512,256]{2,1,0:T(8,128)} %wd_hbm_ref.1), custom_call_target="tpu_custom_call" | custom-call | flops 503316480 | bytes 1572864 | tf_op jit(solution)/shard_map/pallas_call | solution.py:334
  96.9 1.4 shard_map.112
  98.3 7.8 %all-to-all-done.4 = f32[12,16,256]{2,1,0:T(8,128)S(1)} async-done(((f32[12,16,256]{2,1,0:T(8,128)}), f32[12,16,256]{2,1,0:T(8,128)S(1)}, u32[]{:S(2)}, u32[]{:S(2)}) %all-to-all-start.4) | async-done | bytes 196640 | tf_op jit(solution)/shard_map/all_to_all | solution.py:266
  106.0 11.5 %all-gather = f32[768,256]{1,0:T(8,128)S(1)} all-gather(f32[192,256]{1,0:T(8,128)S(1)} %bitcast.11), channel_id=2, replica_groups=mesh['z'=12,'x'=4,'c'=2,'head'=8] {'x'}, dimensions={0}, use_global_device_ids=true | all-gather | bytes 983040 | tf_op jit(solution)/shard_map/all_gather | solution.py:348
  117.6 0.0 all-gather.7.cloned.1.call-done
  117.6 1.9 %shard_map.113 = (f32[128,512]{1,0:T(8,128)S(1)}, f32[128,512]{1,0:T(8,128)S(1)}, f32[8,192,256]{2,1,0:T(8,128)S(1)}, f32[128,256]{1,0:T(8,128)S(1)}, f32[128,256]{1,0:T(8,128)S(1)}) custom-call(f32[4,192,256]{2,1,0:T(8,128)S(1)} %bitcast.8, f32[256,512]{1,0:T(8,128)S(1)} %get-tuple-element.52.pair_ref, f32[4,192,256]{2,1,0:T(8,128)S(1)} %get-tuple-element.53.w_ref, ...), custom_call_target="tpu_custom_call" | custom-call | flops 1207959552 | bytes 2359296 | tf_op jit(solution)/shard_map/pallas_call | solution.py:349
  119.5 9.7 %collective-permute-start.1 = (f32[128,512]{1,0:T(8,128)S(1)}, f32[128,512]{1,0:T(8,128)S(1)}, u32[]{:S(2)}, u32[]{:S(2)}) collective-permute-start(f32[128,512]{1,0:T(8,128)S(1)} %get-tuple-element.55), channel_id=1, source_target_pairs={{0,8},{8,0},{1,9},{9,1},{2,10},{10,2},{3,11},{11,3},{4,12},{12,4},... | collective-permute-start | bytes 786440 | tf_op jit(solution)/shard_map/ppermute | solution.py:265
  129.2 1.9 %shard_map.114 = f32[2,128,256]{2,1,0:T(8,128)} custom-call(f32[128,256]{1,0:T(8,128)S(1)} %get-tuple-element.56.q_ref, f32[128,256]{1,0:T(8,128)S(1)} %get-tuple-element.57.c_ref, f32[8,192,256]{2,1,0:T(8,128)S(1)} %get-tuple-element.58.w_ref, f32[128,256]{1,0:T(8,128)S(1)} %shard_map.111.zero_ref), custom_call_target="tpu_custom_call" | custom-call | flops 503316480 | bytes 1572864 | tf_op jit(solution)/shard_map/pallas_call | solution.py:359
  131.1 0.0 collective-permute-done.1.got_ref
  131.1 0.7 shard_map.115
  (1 shorter events, 0.0 us)
Async XLA Ops:
  7.2 55.0 %all-gather.5.cloned.1.call-start = ((), (), s32[]{:S(2)}) async-start(), calls=%async_computation.5 | async-start | bytes 2359296 | tf_op jit(solution)/shard_map/all_gather | solution.py:305
  8.2 13.7 %collective-permute-start = (f32[128,512]{1,0:T(8,128)S(1)}, f32[128,512]{1,0:T(8,128)S(1)}, u32[]{:S(2)}, u32[]{:S(2)}) collective-permute-start(f32[128,512]{1,0:T(8,128)S(1)} %get-tuple-element.34.own_ref), channel_id=1, source_target_pairs={{0,8},{8,0},{1,9},{9,1},{2,10},{10,2},{3,11},{11,3},{4,12},{12,4},... | collective-permute-start | bytes 786440 | tf_op jit(solution)/shard_map/ppermute | solution.py:265
  57.7 15.4 %all-to-all-start.2 = ((f32[12,16,256]{2,1,0:T(8,128)}), f32[12,16,256]{2,1,0:T(8,128)S(1)}, u32[]{:S(2)}, u32[]{:S(2)}) async-start(f32[12,16,256]{2,1,0:T(8,128)} %shard_map.107), calls=%async_computation.2 | async-start | bytes 393216 | tf_op jit(solution)/shard_map/all_to_all | solution.py:266
  62.1 55.5 %all-gather.7.cloned.1.call-start = ((), (), s32[]{:S(2)}) async-start(), calls=%async_computation.6 | async-start | bytes 1769472 | tf_op jit(solution)/shard_map/all_gather | solution.py:331
  90.4 15.6 %all-to-all-start.4 = ((f32[12,16,256]{2,1,0:T(8,128)}), f32[12,16,256]{2,1,0:T(8,128)S(1)}, u32[]{:S(2)}, u32[]{:S(2)}) async-start(f32[12,16,256]{2,1,0:T(8,128)} %shard_map.110), calls=%async_computation.4 | async-start | bytes 393216 | tf_op jit(solution)/shard_map/all_to_all | solution.py:266
  119.5 11.6 %collective-permute-start.1 = (f32[128,512]{1,0:T(8,128)S(1)}, f32[128,512]{1,0:T(8,128)S(1)}, u32[]{:S(2)}, u32[]{:S(2)}) collective-permute-start(f32[128,512]{1,0:T(8,128)S(1)} %get-tuple-element.55), channel_id=1, source_target_pairs={{0,8},{8,0},{1,9},{9,1},{2,10},{10,2},{3,11},{11,3},{4,12},{12,4},... | collective-permute-start | bytes 786440 | tf_op jit(solution)/shard_map/ppermute | solution.py:265
Sparse Core Ops, SparseCore 0:
  24.1 30.8 all-gather.4
  74.9 28.9 all-gather.6

commit v4 on v3

--- a/solution.py
+++ b/solution.py
@@ -65,7 +65,7 @@
     copies[2].wait()
 
 
-def units_kernel(wg_ref, wu_ref, wd_ref, out_ref, raw_ref, sems):
+def units_kernel(wg_ref, wu_ref, wd_ref, q_ref, c_ref, out_ref, ask_ref, raw_ref, sems):
     nx, rows, width = out_ref.shape
     units = rows // 3
     half = nx * units
@@ -75,6 +75,7 @@
         (wu_ref.at[0, :, pl.ds(start, half)], raw_ref.at[1]),
     ]
     pairs += [(wd_ref.at[0, pl.ds(start + i * units, units)], out_ref.at[i, 2 * units :]) for i in range(nx)]
+    pairs += [(q_ref.at[1], ask_ref.at[:, :width]), (c_ref.at[1], ask_ref.at[:, width:])]
     copies = start_all(pairs, sems)
     for i in range(2):
         copies[i].wait()
@@ -129,13 +130,12 @@
     return total
 
 
-def inner_kernel(own_ref, other_ref, w_ref, q_ref, c_ref, out_ref, piece_ref, ask_ref, pair_ref, kept_ref, sems):
+def inner_kernel(own_ref, other_ref, w_ref, asked_ref, out_ref, piece_ref, ask_ref, pair_ref, kept_ref, sems):
     nx, rows, width = w_ref.shape
     units = rows // 3
     n = nx * units
     tok = own_ref.shape[0]
-    pairs = [(q_ref.at[1], ask_ref.at[:, :width]), (c_ref.at[1], ask_ref.at[:, width:])]
-    pairs += [(own_ref, pair_ref.at[:tok]), (other_ref, pair_ref.at[tok:]), (w_ref, kept_ref)]
+    pairs = [(asked_ref, ask_ref), (own_ref, pair_ref.at[:tok]), (other_ref, pair_ref.at[tok:]), (w_ref, kept_ref)]
     copies = start_all(pairs, sems)
     piece = piece_ref.shape[0]
     start = pl.multiple_of(lax.axis_index("z") * piece, 8)
@@ -152,19 +152,25 @@
         copy.wait()
 
 
-def outer_kernel(rows_ref, w_ref, out_ref, new_ref, sems):
-    copies = start_all([(w_ref, new_ref)], sems)
+def outer_kernel(ask_ref, w_ref, out_ref, new_ref, rows_ref, sems):
     width = w_ref.shape[1]
     units = w_ref.shape[0] // 3
-    step = 256
-    chunks = [
-        (rows_ref[at : at + step, :width], rows_ref[at : at + step, width:])
-        for at in range(0, rows_ref.shape[0], step)
-    ]
-    in_sum, down_sum = weight_grad(split(w_ref[: 2 * units]), split(w_ref[2 * units :]), chunks)
-    out_ref[: 2 * units] = in_sum
-    out_ref[2 * units :] = down_sum
-    copies[0].wait()
+    tokens = ask_ref.shape[0]
+    cuts = [0, 128, *range(256, tokens + 1, 256)]
+    spans = [slice(*pair) for pair in zip(cuts, cuts[1:])]
+    pairs = [(ask_ref.at[span], rows_ref.at[span]) for span in spans]
+    *copies, last = start_all(pairs + [(w_ref, new_ref)], sems)
+    w_in, w_down = split(w_ref[: 2 * units]), split(w_ref[2 * units :])
+    for span, copy in zip(spans, copies):
+        copy.wait()
+        in_sum, down_sum = weight_grad(w_in, w_down, [(rows_ref[span, :width], rows_ref[span, width:])])
+        if span.start == 0:
+            out_ref[: 2 * units] = in_sum
+            out_ref[2 * units :] = down_sum
+        else:
+            out_ref[: 2 * units] += in_sum
+            out_ref[2 * units :] += down_sum
+    last.wait()
 
 
 def query_grad(rows, cots, w_gate, w_up, w_down, up_way, down_way):
@@ -194,15 +200,21 @@
     out_ref[1] = query_grad(q_ref[...], c_ref[...], w_gate, w_up, w_down, NT, NN)
 
 
-def load_kernel(*refs):
-    *refs, sems = refs
-    n = len(refs) // 2
-    for copy in start_all(list(zip(refs[:n], refs[n:])), sems):
-        copy.wait()
+def prepare_kernel(
+    pair_hbm_ref, w_hbm_ref, pair_ref, w_ref, gate_ref, up_ref, grad_ref, sems
+):
+    for copy in start_all([(pair_hbm_ref, pair_ref), (w_hbm_ref, w_ref)], sems):
+        copy.wait()
+    width = w_ref.shape[2]
+    w_gate, w_up, w_down = [split(w) for w in parts(w_ref, w_ref.shape[1] // 3)]
+    rows, cots = split(pair_ref[:, :width]), split(pair_ref[:, width:])
+    gate_ref[...] = dot3(rows, w_gate, NT)
+    up_ref[...] = dot3(rows, w_up, NT)
+    grad_ref[...] = dot3(cots, w_down, NT)
 
 
 def final_kernel(
-    d_ref, pair_ref, w_ref, new_ref, q_ref, c_ref, mine_ref, theirs_ref, new_out_ref, q_out_ref, c_out_ref, sems
+    d_ref, pair_ref, w_ref, gate_ref, up_ref, grad_ref, new_ref, q_ref, c_ref, mine_ref, theirs_ref, new_out_ref, q_out_ref, c_out_ref, sems
 ):
     copies = start_all([(new_ref, new_out_ref), (q_ref.at[1], q_out_ref), (c_ref.at[1], c_out_ref)], sems)
     width = d_ref.shape[2]
@@ -210,8 +222,7 @@
     d_gate, d_up, d_down = [split(d) for d in parts(d_ref, units)]
     w_gate, w_up, w_down = [split(w) for w in parts(w_ref, units)]
     rows, cots = split(pair_ref[:, :width]), split(pair_ref[:, width:])
-    gate, up_part = dot3(rows, w_gate, NT), dot3(rows, w_up, NT)
-    hidden_grad = dot3(cots, w_down, NT)
+    gate, up_part, hidden_grad = gate_ref[...], up_ref[...], grad_ref[...]
     sigma, active, slope = gates(gate)
     bend = sigma * (1.0 - sigma) * (2.0 + gate * (1.0 - 2.0 * sigma))
     steep = slope * up_part
@@ -281,53 +292,44 @@
         ],
     )(hold(keys), hold(values), hold(rates.reshape(1, tok)))
     other = swap(own)
-    w_rows = call(
+    w_rows, ask = call(
         units_kernel,
-        f32(NX, 3 * units, width),
+        [f32(NX, 3 * units, width), f32(tok, 2 * width)],
         0,
         2 * n_w,
-        in_specs=[there] * 3,
-        out_specs=here,
-        scratch_shapes=[pltpu.VMEM((2, width, half), jnp.float32), pltpu.SemaphoreType.DMA((2 + NX,))],
-    )(hold(after(w_gate, own)), hold(w_up), hold(w_down))
+        in_specs=[there] * 5,
+        out_specs=[here] * 2,
+        scratch_shapes=[pltpu.VMEM((2, width, half), jnp.float32), pltpu.SemaphoreType.DMA((4 + NX,))],
+    )(*[hold(a) for a in (after(w_gate, own), w_up, w_down, queries, grad_out)])
 
     pair_shape = pltpu.HBM((2 * tok, 2 * width), jnp.float32)
+    ask_shape = pltpu.HBM((tok, 2 * width), jnp.float32)
     kept_shape = pltpu.HBM((NX, 3 * units, width), jnp.float32)
     inner, w_piece, ask, pair, kept = call(
         inner_kernel,
-        [f32(NX, 3 * units, width), f32(piece, width), f32(tok, 2 * width), pair_shape, kept_shape],
+        [f32(NX, 3 * units, width), f32(piece, width), ask_shape, pair_shape, kept_shape],
         36 * n_mul,
         2 * n_w,
-        in_specs=[here, here, here, there, there],
-        out_specs=[here, here, here, there, there],
-        scratch_shapes=[pltpu.SemaphoreType.DMA((5,))],
-    )(own, other, w_rows, hold(queries), hold(grad_out))
+        in_specs=[here] * 4,
+        out_specs=[here, here, there, there, there],
+        scratch_shapes=[pltpu.SemaphoreType.DMA((4,))],
+    )(own, other, w_rows, ask)
     ask = lax.all_gather(ask, ("x", "c"), axis=0, tiled=True)
     inner = lax.all_to_all(inner, "x", 0, 0)
     inner = call(row_sum_kernel, f32(3 * units, width), 0, 2 * n_w)(inner)
     pieces = f32(n_z, piece, width)
     new = call(functools.partial(update_kernel, scale), pieces, 0, n_w)(exchange(inner), w_piece)
-    load = lambda *args: call(
-        load_kernel,
-        [f32(*a.shape) for a in args],
-        0,
-        8 * sum(a.size for a in args),
-        in_specs=[there] * len(args),
-        out_specs=[here] * len(args),
-        scratch_shapes=[pltpu.SemaphoreType.DMA((len(args),))],
-    )(*[hold(a) for a in args])
-    (ask,) = load(after(ask, new))
-    new, ask = both(exchange(new).reshape(3 * units, width), ask)
+    new = exchange(new).reshape(3 * units, width)
 
     outer, new = call(
         outer_kernel,
         [f32(3 * units, width), pltpu.HBM((3 * units, width), jnp.float32)],
         36 * n_mul,
         64 * tok * width,
-        in_specs=[here, here],
+        in_specs=[there, here],
         out_specs=[here, there],
-        scratch_shapes=[pltpu.SemaphoreType.DMA((1,))],
-    )(ask, new)
+        scratch_shapes=[pltpu.VMEM(ask.shape, jnp.float32), pltpu.SemaphoreType.DMA((6,))],
+    )(hold(ask), new)
     new_all = lax.all_gather(new, ("x", "c"), axis=0, tiled=False)
     outer = call(total_kernel, pieces, 0, n_w)(exchange(outer))
     vmem = lambda *shape: pltpu.VMEM(shape, jnp.float32)
@@ -343,7 +345,15 @@
             pltpu.SemaphoreType.DMA((5,)),
         ],
     )(*[hold(a) for a in (after(queries, outer), grad_out, w_gate, w_up, w_down)])
-    loaded = load(after(pair, zero), kept)
+    loaded = call(
+        prepare_kernel,
+        [f32(2 * tok, 2 * width), f32(NX, 3 * units, width)] + [f32(2 * tok, half)] * 3,
+        18 * n_mul,
+        4 * n_w,
+        in_specs=[there] * 2,
+        out_specs=[here] * 5,
+        scratch_shapes=[pltpu.SemaphoreType.DMA((2,))],
+    )(hold(after(pair, zero)), hold(kept))
     outer, loaded = both(exchange(outer).reshape(3 * units, width), loaded)
     d_all, new_all = both(lax.all_gather(outer, "x", axis=0, tiled=False), new_all)
     mine, theirs, *ones = call(
@@ -351,7 +361,7 @@
         [f32(tok, 2 * width)] * 2 + [f32(*new_all.shape), f32(tok, width), f32(tok, width)],
         72 * n_mul,
         3 * n_w,
-        in_specs=[here, here, here, there, there, there],
+        in_specs=[here] * 6 + [there] * 3,
         out_specs=[here] * 5,
         scratch_shapes=[pltpu.SemaphoreType.DMA((3,))],
     )(d_all, *loaded, *[hold(a) for a in (new_all, queries, grad_out)])

time: 139 us -> 139 us (level)
  blocking collectives: 59.4 us -> 74.2 us
  waiting for transfers between devices: 17.2 us -> 7.33 us
  starting transfers between devices: 30 us -> 26 us
    all_to_all x2 -> x3, blocking collectives: 33.5 us -> 48.5 us  [body(): exchange = lambda x: lax.all_to_all(x.reshape(n_z, piece, width), 'z', 0, 0)]
    all_to_all x2 -> x1, waiting for transfers between devices: 17.2 us -> 7.29 us  [body(): exchange = lambda x: lax.all_to_all(x.reshape(n_z, piece, width), 'z', 0, 0)]
    all_to_all x2 -> x1, starting transfers between devices: 7.86 us -> 3.53 us  [body(): exchange = lambda x: lax.all_to_all(x.reshape(n_z, piece, width), 'z', 0, 0)]
    pallas_call x4 -> x3, Pallas kernels: 6.26 us -> 4.37 us  [the longest x1 1.86 us: body(): call(prepare_kernel, [f32(2 * tok, 2 * width), f32(NX, 3 * units, width)]...]
    pallas_call x1, Pallas kernels: 1.64 us -> 3.27 us  [body(): call(outer_kernel, [f32(3 * units, width), pltpu.HBM((3 * units, width),...]
  transfers between devices with their start and end apart: 6 -> 5, of which waited for: 2 -> 1; matrix products, arithmetic and copies ran while one was open for 0% -> 0% of each run, Pallas kernels for 8% -> 6%
where the time goes in v4:
time: 139 us; the launch traced here: 138 us
  blocking collectives  74.2 us (53%)
  starting transfers between devices  26 us (19%)
  Pallas kernels  16.6 us (12%)
  between operations  14.1 us (10%)
  waiting for transfers between devices  7.33 us (5%)
    all_to_all x3, blocking collectives, body(): exchange = lambda x: lax.all_to_all(x.reshape(n_z, piece, width), 'z', 0, 0)  48.5 us
    ppermute x2, starting transfers between devices, body(): lax.ppermute(x, 'c', [(i, (i + 1) % NC) for i in range(NC)])  22.4 us
    all_to_all x1, blocking collectives, body(): inner = lax.all_to_all(inner, 'x', 0, 0)  14.4 us
    all_gather x1, blocking collectives, body(): lax.all_gather(outer, 'x', axis=0, tiled=False)  11.2 us
    all_to_all x1, waiting for transfers between devices, body(): exchange = lambda x: lax.all_to_all(x.reshape(n_z, piece, width), 'z', 0, 0)  7.29 us
    all_to_all x1, starting transfers between devices, body(): exchange = lambda x: lax.all_to_all(x.reshape(n_z, piece, width), 'z', 0, 0)  3.53 us
    pallas_call x1, Pallas kernels, body(): call(outer_kernel, [f32(3 * units, width), pltpu.HBM((3 * units, width),...  3.27 us
    pallas_call x1, Pallas kernels, body(): call(zero_kernel, f32(tok, width), 30 * n_mul, 2 * n_w, in_specs=[there]...  2.9 us
  transfers between devices with their start and end apart: 5, of which 1 were waited for; matrix products, arithmetic and copies ran while one was open for 0% of the time, Pallas kernels for 6%

profile of v4, /device:TPU:1, one launch (start us, length us, event | category | flops | bytes accessed | tf_op | source)
XLA Modules:
  0.0 138.2 jit_solution(11952159955251788270)
XLA Ops:
  7.2 0.0 all-gather.5.cloned.1.call-start
  7.2 1.0 shard_map.103
  8.2 12.4 %collective-permute-start = (f32[128,512]{1,0:T(8,128)S(1)}, f32[128,512]{1,0:T(8,128)S(1)}, u32[]{:S(2)}, u32[]{:S(2)}) collective-permute-start(f32[128,512]{1,0:T(8,128)S(1)} %get-tuple-element.39.own_ref), channel_id=1, source_target_pairs={{0,8},{8,0},{1,9},{9,1},{2,10},{10,2},{3,11},{11,3},{4,12},{12,4},... | collective-permute-start | bytes 786440 | tf_op jit(solution)/shard_map/ppermute | solution.py:276
  20.7 1.3 shard_map.104
  22.0 0.0 collective-permute-done.other_ref
  22.0 1.2 shard_map.105
  23.2 0.0 all-gather.5.cloned.1.call-update
  23.2 0.0 all-gather.7.cloned.1.call-start
  23.3 14.4 %all_to_all.25.in_ref = f32[4,192,256]{2,1,0:T(8,128)S(1)} all-to-all(f32[4,192,256]{2,1,0:T(8,128)S(1)} %get-tuple-element.44), channel_id=1, replica_groups=mesh['z'=12,'x'=4,'c'=2,'head'=8] {'x'}, dimensions={0} | all-to-all | bytes 1572864 | tf_op jit(solution)/shard_map/all_to_all | solution.py:318
  37.7 18.6 %all_to_all.26.in_ref = f32[12,16,256]{2,1,0:T(8,128)S(1)} all-to-all(f32[12,16,256]{2,1,0:T(8,128)S(1)} %bitcast.9), channel_id=1, replica_groups=mesh['z'=12,'x'=4,'c'=2,'head'=8] {'z'}, dimensions={0} | all-to-all | bytes 393216 | tf_op jit(solution)/shard_map/all_to_all | solution.py:277
  56.3 15.2 %all_to_all.27 = f32[12,16,256]{2,1,0:T(8,128)S(1)} all-to-all(f32[12,16,256]{2,1,0:T(8,128)S(1)} %shard_map.107), channel_id=1, replica_groups=mesh['z'=12,'x'=4,'c'=2,'head'=8] {'z'}, dimensions={0} | all-to-all | bytes 393216 | tf_op jit(solution)/shard_map/all_to_all | solution.py:277
  71.6 0.0 all-gather.5.cloned.1.call-done.ask_ref
  71.6 3.3 %shard_map.108 = (f32[192,256]{1,0:T(8,128)S(1)}, f32[192,256]{1,0:T(8,128)}) custom-call(f32[1024,512]{1,0:T(8,128)} %all-gather.5.cloned.1.call-done.ask_ref, f32[192,256]{1,0:T(8,128)S(1)} %bitcast.8), custom_call_target="tpu_custom_call" | custom-call | flops 603979776 | bytes 2097152 | tf_op jit(solution)/shard_map/pallas_call | solution.py:324
  74.9 0.0 all-gather.7.cloned.1.call-update
  74.9 14.7 %all_to_all.28.in_ref = f32[12,16,256]{2,1,0:T(8,128)S(1)} all-to-all(f32[12,16,256]{2,1,0:T(8,128)S(1)} %bitcast.10), channel_id=1, replica_groups=mesh['z'=12,'x'=4,'c'=2,'head'=8] {'z'}, dimensions={0} | all-to-all | bytes 393216 | tf_op jit(solution)/shard_map/all_to_all | solution.py:277
  89.6 0.7 shard_map.109
  90.3 3.5 %all-to-all-start.4 = ((f32[12,16,256]{2,1,0:T(8,128)}), f32[12,16,256]{2,1,0:T(8,128)S(1)}, u32[]{:S(2)}, u32[]{:S(2)}) async-start(f32[12,16,256]{2,1,0:T(8,128)} %shard_map.109), calls=%async_computation.4 | async-start | bytes 393216 | tf_op jit(solution)/shard_map/all_to_all | solution.py:277
  93.9 2.9 %shard_map.110.zero_ref = f32[128,256]{1,0:T(8,128)S(1)} custom-call(f32[2,128,256]{2,1,0:T(8,128)} %q_ref.3, f32[2,128,256]{2,1,0:T(8,128)} %c_ref.3, f32[1,256,512]{2,1,0:T(8,128)} %wg_hbm_ref.1, f32[1,256,512]{2,1,0:T(8,128)} %wu_hbm_ref.1, f32[1,512,256]{2,1,0:T(8,128)} %wd_hbm_ref.1), custom_call_target="tpu_custom_call" | custom-call | flops 503316480 | bytes 1572864 | tf_op jit(solution)/shard_map/pallas_call | solution.py:336
  96.8 1.9 %shard_map.111 = (f32[256,512]{1,0:T(8,128)S(1)}, f32[4,192,256]{2,1,0:T(8,128)S(1)}, f32[256,256]{1,0:T(8,128)S(1)}, f32[256,256]{1,0:T(8,128)S(1)}, f32[256,256]{1,0:T(8,128)S(1)}) custom-call(f32[256,512]{1,0:T(8,128)} %get-tuple-element.49.pair_hbm_ref, f32[4,192,256]{2,1,0:T(8,128)} %get-tuple-element.50.w_hbm_ref), custom_call_target="tpu_custom_call" | custom-call | flops 301989888 | bytes 3145728 | tf_op jit(solution)/shard_map/pallas_call | solution.py:348
  98.6 7.3 %all-to-all-done.4 = f32[12,16,256]{2,1,0:T(8,128)S(1)} async-done(((f32[12,16,256]{2,1,0:T(8,128)}), f32[12,16,256]{2,1,0:T(8,128)S(1)}, u32[]{:S(2)}, u32[]{:S(2)}) %all-to-all-start.4) | async-done | bytes 196640 | tf_op jit(solution)/shard_map/all_to_all | solution.py:277
  105.9 11.2 %all-gather = f32[768,256]{1,0:T(8,128)S(1)} all-gather(f32[192,256]{1,0:T(8,128)S(1)} %bitcast.12), channel_id=2, replica_groups=mesh['z'=12,'x'=4,'c'=2,'head'=8] {'x'}, dimensions={0}, use_global_device_ids=true | all-gather | bytes 983040 | tf_op jit(solution)/shard_map/all_gather | solution.py:358
  117.2 0.0 all-gather.7.cloned.1.call-done
  117.2 1.6 %shard_map.112 = (f32[128,512]{1,0:T(8,128)S(1)}, f32[128,512]{1,0:T(8,128)S(1)}, f32[8,192,256]{2,1,0:T(8,128)S(1)}, f32[128,256]{1,0:T(8,128)S(1)}, f32[128,256]{1,0:T(8,128)S(1)}) custom-call(f32[4,192,256]{2,1,0:T(8,128)S(1)} %bitcast.7, f32[256,512]{1,0:T(8,128)S(1)} %get-tuple-element.59.pair_ref, f32[4,192,256]{2,1,0:T(8,128)S(1)} %get-tuple-element.60.w_ref, ...), custom_call_target="tpu_custom_call" | custom-call | flops 1207959552 | bytes 2359296 | tf_op jit(solution)/shard_map/pallas_call | solution.py:359
  118.8 10.0 %collective-permute-start.1 = (f32[128,512]{1,0:T(8,128)S(1)}, f32[128,512]{1,0:T(8,128)S(1)}, u32[]{:S(2)}, u32[]{:S(2)}) collective-permute-start(f32[128,512]{1,0:T(8,128)S(1)} %get-tuple-element.65), channel_id=1, source_target_pairs={{0,8},{8,0},{1,9},{9,1},{2,10},{10,2},{3,11},{11,3},{4,12},{12,4},... | collective-permute-start | bytes 786440 | tf_op jit(solution)/shard_map/ppermute | solution.py:276
  128.7 1.9 %shard_map.113 = f32[2,128,256]{2,1,0:T(8,128)} custom-call(f32[128,256]{1,0:T(8,128)S(1)} %get-tuple-element.66.q_ref, f32[128,256]{1,0:T(8,128)S(1)} %get-tuple-element.67.c_ref, f32[8,192,256]{2,1,0:T(8,128)S(1)} %get-tuple-element.68.w_ref, f32[128,256]{1,0:T(8,128)S(1)} %shard_map.110.zero_ref), custom_call_target="tpu_custom_call" | custom-call | flops 503316480 | bytes 1572864 | tf_op jit(solution)/shard_map/pallas_call | solution.py:369
  130.7 0.0 collective-permute-done.1.got_ref
  130.7 0.7 shard_map.114
  (2 shorter events, 0.1 us)
Async XLA Ops:
  7.2 64.4 %all-gather.5.cloned.1.call-start = ((), (), s32[]{:S(2)}) async-start(), calls=%async_computation.5 | async-start | bytes 2359296 | tf_op jit(solution)/shard_map/all_gather | solution.py:317
  8.2 13.8 %collective-permute-start = (f32[128,512]{1,0:T(8,128)S(1)}, f32[128,512]{1,0:T(8,128)S(1)}, u32[]{:S(2)}, u32[]{:S(2)}) collective-permute-start(f32[128,512]{1,0:T(8,128)S(1)} %get-tuple-element.39.own_ref), channel_id=1, source_target_pairs={{0,8},{8,0},{1,9},{9,1},{2,10},{10,2},{3,11},{11,3},{4,12},{12,4},... | collective-permute-start | bytes 786440 | tf_op jit(solution)/shard_map/ppermute | solution.py:276
  23.2 93.9 %all-gather.7.cloned.1.call-start = ((), (), s32[]{:S(2)}) async-start(), calls=%async_computation.6 | async-start | bytes 1769472 | tf_op jit(solution)/shard_map/all_gather | solution.py:333
  90.3 15.6 %all-to-all-start.4 = ((f32[12,16,256]{2,1,0:T(8,128)}), f32[12,16,256]{2,1,0:T(8,128)S(1)}, u32[]{:S(2)}, u32[]{:S(2)}) async-start(f32[12,16,256]{2,1,0:T(8,128)} %shard_map.109), calls=%async_computation.4 | async-start | bytes 393216 | tf_op jit(solution)/shard_map/all_to_all | solution.py:277
  118.8 11.9 %collective-permute-start.1 = (f32[128,512]{1,0:T(8,128)S(1)}, f32[128,512]{1,0:T(8,128)S(1)}, u32[]{:S(2)}, u32[]{:S(2)}) collective-permute-start(f32[128,512]{1,0:T(8,128)S(1)} %get-tuple-element.65), channel_id=1, source_target_pairs={{0,8},{8,0},{1,9},{9,1},{2,10},{10,2},{3,11},{11,3},{4,12},{12,4},... | collective-permute-start | bytes 786440 | tf_op jit(solution)/shard_map/ppermute | solution.py:276
Sparse Core Ops, SparseCore 0:
  23.3 30.8 all-gather.4
  75.0 28.9 all-gather.6

commit v5 on v4

--- a/solution.py
+++ b/solution.py
@@ -152,25 +152,25 @@
         copy.wait()
 
 
-def outer_kernel(ask_ref, w_ref, out_ref, new_ref, rows_ref, sems):
+def load_kernel(from_ref, to_ref, sems):
+    n = to_ref.shape[0] // 2
+    for copy in start_all([(from_ref.at[:n], to_ref.at[:n]), (from_ref.at[n:], to_ref.at[n:])], sems):
+        copy.wait()
+
+
+def outer_kernel(rows_ref, w_ref, out_ref, new_ref, sems):
+    copies = start_all([(w_ref, new_ref)], sems)
     width = w_ref.shape[1]
     units = w_ref.shape[0] // 3
-    tokens = ask_ref.shape[0]
-    cuts = [0, 128, *range(256, tokens + 1, 256)]
-    spans = [slice(*pair) for pair in zip(cuts, cuts[1:])]
-    pairs = [(ask_ref.at[span], rows_ref.at[span]) for span in spans]
-    *copies, last = start_all(pairs + [(w_ref, new_ref)], sems)
-    w_in, w_down = split(w_ref[: 2 * units]), split(w_ref[2 * units :])
-    for span, copy in zip(spans, copies):
-        copy.wait()
-        in_sum, down_sum = weight_grad(w_in, w_down, [(rows_ref[span, :width], rows_ref[span, width:])])
-        if span.start == 0:
-            out_ref[: 2 * units] = in_sum
-            out_ref[2 * units :] = down_sum
-        else:
-            out_ref[: 2 * units] += in_sum
-            out_ref[2 * units :] += down_sum
-    last.wait()
+    step = 256
+    chunks = [
+        (rows_ref[at : at + step, :width], rows_ref[at : at + step, width:])
+        for at in range(0, rows_ref.shape[0], step)
+    ]
+    in_sum, down_sum = weight_grad(split(w_ref[: 2 * units]), split(w_ref[2 * units :]), chunks)
+    out_ref[: 2 * units] = in_sum
+    out_ref[2 * units :] = down_sum
+    copies[0].wait()
 
 
 def query_grad(rows, cots, w_gate, w_up, w_down, up_way, down_way):
@@ -319,17 +319,26 @@
     inner = call(row_sum_kernel, f32(3 * units, width), 0, 2 * n_w)(inner)
     pieces = f32(n_z, piece, width)
     new = call(functools.partial(update_kernel, scale), pieces, 0, n_w)(exchange(inner), w_piece)
-    new = exchange(new).reshape(3 * units, width)
+    ask = call(
+        load_kernel,
+        f32(*ask.shape),
+        0,
+        8 * ask.size,
+        in_specs=[there],
+        out_specs=here,
+        scratch_shapes=[pltpu.SemaphoreType.DMA((2,))],
+    )(hold(after(ask, new)))
+    new, ask = both(exchange(new).reshape(3 * units, width), ask)
 
     outer, new = call(
         outer_kernel,
         [f32(3 * units, width), pltpu.HBM((3 * units, width), jnp.float32)],
         36 * n_mul,
         64 * tok * width,
-        in_specs=[there, here],
+        in_specs=[here, here],
         out_specs=[here, there],
-        scratch_shapes=[pltpu.VMEM(ask.shape, jnp.float32), pltpu.SemaphoreType.DMA((6,))],
-    )(hold(ask), new)
+        scratch_shapes=[pltpu.SemaphoreType.DMA((1,))],
+    )(ask, new)
     new_all = lax.all_gather(new, ("x", "c"), axis=0, tiled=False)
     outer = call(total_kernel, pieces, 0, n_w)(exchange(outer))
     vmem = lambda *shape: pltpu.VMEM(shape, jnp.float32)

time: 139 us -> 138 us (level)
  blocking collectives: 74.2 us -> 59.5 us
  waiting for transfers between devices: 7.33 us -> 16.7 us
  starting transfers between devices: 26 us -> 30 us
    all_to_all x3 -> x2, blocking collectives: 48.5 us -> 33.5 us  [body(): exchange = lambda x: lax.all_to_all(x.reshape(n_z, piece, width), 'z', 0, 0)]
    all_to_all x1 -> x2, waiting for transfers between devices: 7.29 us -> 16.7 us  [body(): exchange = lambda x: lax.all_to_all(x.reshape(n_z, piece, width), 'z', 0, 0)]
    all_to_all x1 -> x2, starting transfers between devices: 3.53 us -> 7.9 us  [body(): exchange = lambda x: lax.all_to_all(x.reshape(n_z, piece, width), 'z', 0, 0)]
    pallas_call x1, Pallas kernels: 3.27 us -> 1.64 us  [body(): call(outer_kernel, [f32(3 * units, width), pltpu.HBM((3 * units, width),...]
    pallas_call x0 -> x1, Pallas kernels: none -> 1.56 us  [body(): call(load_kernel, f32(*ask.shape), 0, 8 * ask.size, in_specs=[there], out...]
  transfers between devices with their start and end apart: 5 -> 6, of which waited for: 1 -> 2; matrix products, arithmetic and copies ran while one was open for 0% -> 0% of each run, Pallas kernels for 6% -> 8%
where the time goes in v5:
time: 138 us
  blocking collectives  59.5 us (43%)
  starting transfers between devices  30 us (22%)
  Pallas kernels  17.3 us (13%)
  waiting for transfers between devices  16.7 us (12%)
  between operations  14.2 us (10%)
    all_to_all x2, blocking collectives, body(): exchange = lambda x: lax.all_to_all(x.reshape(n_z, piece, width), 'z', 0, 0)  33.5 us
    ppermute x2, starting transfers between devices, body(): lax.ppermute(x, 'c', [(i, (i + 1) % NC) for i in range(NC)])  22 us
    all_to_all x2, waiting for transfers between devices, body(): exchange = lambda x: lax.all_to_all(x.reshape(n_z, piece, width), 'z', 0, 0)  16.7 us
    all_to_all x1, blocking collectives, body(): inner = lax.all_to_all(inner, 'x', 0, 0)  14.4 us
    all_gather x1, blocking collectives, body(): lax.all_gather(outer, 'x', axis=0, tiled=False)  11.6 us
    all_to_all x2, starting transfers between devices, body(): exchange = lambda x: lax.all_to_all(x.reshape(n_z, piece, width), 'z', 0, 0)  7.9 us
    pallas_call x1, Pallas kernels, body(): call(zero_kernel, f32(tok, width), 30 * n_mul, 2 * n_w, in_specs=[there]...  2.92 us
  transfers between devices with their start and end apart: 6, of which 2 were waited for; matrix products, arithmetic and copies ran while one was open for 0% of the time, Pallas kernels for 8%

profile of v5, /device:TPU:1, one launch (start us, length us, event | category | flops | bytes accessed | tf_op | source)
XLA Modules:
  0.0 137.6 jit_solution(16410954135470485985)
XLA Ops:
  7.2 0.0 all-gather.5.cloned.1.call-start
  7.2 1.0 shard_map.103
  8.2 12.4 %collective-permute-start = (f32[128,512]{1,0:T(8,128)S(1)}, f32[128,512]{1,0:T(8,128)S(1)}, u32[]{:S(2)}, u32[]{:S(2)}) collective-permute-start(f32[128,512]{1,0:T(8,128)S(1)} %get-tuple-element.42.own_ref), channel_id=1, source_target_pairs={{0,8},{8,0},{1,9},{9,1},{2,10},{10,2},{3,11},{11,3},{4,12},{12,4},... | collective-permute-start | bytes 786440 | tf_op jit(solution)/shard_map/ppermute | solution.py:276
  20.7 1.3 shard_map.104
  22.0 0.0 collective-permute-done.other_ref
  22.0 1.2 shard_map.105
  23.2 0.0 all-gather.5.cloned.1.call-update
  23.2 14.4 %all_to_all.25.in_ref = f32[4,192,256]{2,1,0:T(8,128)S(1)} all-to-all(f32[4,192,256]{2,1,0:T(8,128)S(1)} %get-tuple-element.46), channel_id=1, replica_groups=mesh['z'=12,'x'=4,'c'=2,'head'=8] {'x'}, dimensions={0} | all-to-all | bytes 1572864 | tf_op jit(solution)/shard_map/all_to_all | solution.py:318
  37.7 18.6 %all_to_all.26.in_ref = f32[12,16,256]{2,1,0:T(8,128)S(1)} all-to-all(f32[12,16,256]{2,1,0:T(8,128)S(1)} %bitcast.9), channel_id=1, replica_groups=mesh['z'=12,'x'=4,'c'=2,'head'=8] {'z'}, dimensions={0} | all-to-all | bytes 393216 | tf_op jit(solution)/shard_map/all_to_all | solution.py:277
  56.3 0.7 shard_map.107
  57.0 4.4 %all-to-all-start.2 = ((f32[12,16,256]{2,1,0:T(8,128)}), f32[12,16,256]{2,1,0:T(8,128)S(1)}, u32[]{:S(2)}, u32[]{:S(2)}) async-start(f32[12,16,256]{2,1,0:T(8,128)} %shard_map.107), calls=%async_computation.2 | async-start | bytes 393216 | tf_op jit(solution)/shard_map/all_to_all | solution.py:277
  61.3 0.0 all-gather.7.cloned.1.call-start
  61.4 0.0 all-gather.5.cloned.1.call-done.from_ref
  61.4 1.6 %shard_map.108.rows_ref = f32[1024,512]{1,0:T(8,128)S(1)} custom-call(f32[1024,512]{1,0:T(8,128)} %all-gather.5.cloned.1.call-done.from_ref), custom_call_target="tpu_custom_call" | custom-call | bytes 4194304 | tf_op jit(solution)/shard_map/pallas_call | solution.py:322
  63.0 9.4 %all-to-all-done.2 = f32[12,16,256]{2,1,0:T(8,128)S(1)} async-done(((f32[12,16,256]{2,1,0:T(8,128)}), f32[12,16,256]{2,1,0:T(8,128)S(1)}, u32[]{:S(2)}, u32[]{:S(2)}) %all-to-all-start.2) | async-done | bytes 196640 | tf_op jit(solution)/shard_map/all_to_all | solution.py:277
  72.4 1.6 %shard_map.109 = (f32[192,256]{1,0:T(8,128)S(1)}, f32[192,256]{1,0:T(8,128)}) custom-call(f32[1024,512]{1,0:T(8,128)S(1)} %shard_map.108.rows_ref, f32[192,256]{1,0:T(8,128)S(1)} %bitcast.8), custom_call_target="tpu_custom_call" | custom-call | flops 603979776 | bytes 2097152 | tf_op jit(solution)/shard_map/pallas_call | solution.py:333
  74.1 0.0 all-gather.7.cloned.1.call-update
  74.1 14.9 %all_to_all.27.in_ref = f32[12,16,256]{2,1,0:T(8,128)S(1)} all-to-all(f32[12,16,256]{2,1,0:T(8,128)S(1)} %bitcast.10), channel_id=1, replica_groups=mesh['z'=12,'x'=4,'c'=2,'head'=8] {'z'}, dimensions={0} | all-to-all | bytes 393216 | tf_op jit(solution)/shard_map/all_to_all | solution.py:277
  89.0 0.7 shard_map.110
  89.7 3.5 %all-to-all-start.4 = ((f32[12,16,256]{2,1,0:T(8,128)}), f32[12,16,256]{2,1,0:T(8,128)S(1)}, u32[]{:S(2)}, u32[]{:S(2)}) async-start(f32[12,16,256]{2,1,0:T(8,128)} %shard_map.110), calls=%async_computation.4 | async-start | bytes 393216 | tf_op jit(solution)/shard_map/all_to_all | solution.py:277
  93.2 2.9 %shard_map.111.zero_ref = f32[128,256]{1,0:T(8,128)S(1)} custom-call(f32[2,128,256]{2,1,0:T(8,128)} %q_ref.3, f32[2,128,256]{2,1,0:T(8,128)} %c_ref.3, f32[1,256,512]{2,1,0:T(8,128)} %wg_hbm_ref.1, f32[1,256,512]{2,1,0:T(8,128)} %wu_hbm_ref.1, f32[1,512,256]{2,1,0:T(8,128)} %wd_hbm_ref.1), custom_call_target="tpu_custom_call" | custom-call | flops 503316480 | bytes 1572864 | tf_op jit(solution)/shard_map/pallas_call | solution.py:345
  96.2 1.9 %shard_map.112 = (f32[256,512]{1,0:T(8,128)S(1)}, f32[4,192,256]{2,1,0:T(8,128)S(1)}, f32[256,256]{1,0:T(8,128)S(1)}, f32[256,256]{1,0:T(8,128)S(1)}, f32[256,256]{1,0:T(8,128)S(1)}) custom-call(f32[256,512]{1,0:T(8,128)} %get-tuple-element.55.pair_hbm_ref, f32[4,192,256]{2,1,0:T(8,128)} %get-tuple-element.56.w_hbm_ref), custom_call_target="tpu_custom_call" | custom-call | flops 301989888 | bytes 3145728 | tf_op jit(solution)/shard_map/pallas_call | solution.py:357
  98.1 7.2 %all-to-all-done.4 = f32[12,16,256]{2,1,0:T(8,128)S(1)} async-done(((f32[12,16,256]{2,1,0:T(8,128)}), f32[12,16,256]{2,1,0:T(8,128)S(1)}, u32[]{:S(2)}, u32[]{:S(2)}) %all-to-all-start.4) | async-done | bytes 196640 | tf_op jit(solution)/shard_map/all_to_all | solution.py:277
  105.3 11.6 %all-gather = f32[768,256]{1,0:T(8,128)S(1)} all-gather(f32[192,256]{1,0:T(8,128)S(1)} %bitcast.12), channel_id=2, replica_groups=mesh['z'=12,'x'=4,'c'=2,'head'=8] {'x'}, dimensions={0}, use_global_device_ids=true | all-gather | bytes 983040 | tf_op jit(solution)/shard_map/all_gather | solution.py:367
  116.9 0.0 all-gather.7.cloned.1.call-done
  116.9 1.6 %shard_map.113 = (f32[128,512]{1,0:T(8,128)S(1)}, f32[128,512]{1,0:T(8,128)S(1)}, f32[8,192,256]{2,1,0:T(8,128)S(1)}, f32[128,256]{1,0:T(8,128)S(1)}, f32[128,256]{1,0:T(8,128)S(1)}) custom-call(f32[4,192,256]{2,1,0:T(8,128)S(1)} %bitcast.7, f32[256,512]{1,0:T(8,128)S(1)} %get-tuple-element.65.pair_ref, f32[4,192,256]{2,1,0:T(8,128)S(1)} %get-tuple-element.66.w_ref, ...), custom_call_target="tpu_custom_call" | custom-call | flops 1207959552 | bytes 2359296 | tf_op jit(solution)/shard_map/pallas_call | solution.py:368
  118.5 9.6 %collective-permute-start.1 = (f32[128,512]{1,0:T(8,128)S(1)}, f32[128,512]{1,0:T(8,128)S(1)}, u32[]{:S(2)}, u32[]{:S(2)}) collective-permute-start(f32[128,512]{1,0:T(8,128)S(1)} %get-tuple-element.71), channel_id=1, source_target_pairs={{0,8},{8,0},{1,9},{9,1},{2,10},{10,2},{3,11},{11,3},{4,12},{12,4},... | collective-permute-start | bytes 786440 | tf_op jit(solution)/shard_map/ppermute | solution.py:276
  128.1 1.9 %shard_map.114 = f32[2,128,256]{2,1,0:T(8,128)} custom-call(f32[128,256]{1,0:T(8,128)S(1)} %get-tuple-element.72.q_ref, f32[128,256]{1,0:T(8,128)S(1)} %get-tuple-element.73.c_ref, f32[8,192,256]{2,1,0:T(8,128)S(1)} %get-tuple-element.74.w_ref, f32[128,256]{1,0:T(8,128)S(1)} %shard_map.111.zero_ref), custom_call_target="tpu_custom_call" | custom-call | flops 503316480 | bytes 1572864 | tf_op jit(solution)/shard_map/pallas_call | solution.py:378
  130.1 0.0 collective-permute-done.1.got_ref
  130.1 0.7 shard_map.115
  (1 shorter events, 0.0 us)
Async XLA Ops:
  7.2 54.2 %all-gather.5.cloned.1.call-start = ((), (), s32[]{:S(2)}) async-start(), calls=%async_computation.5 | async-start | bytes 2359296 | tf_op jit(solution)/shard_map/all_gather | solution.py:317
  8.2 13.8 %collective-permute-start = (f32[128,512]{1,0:T(8,128)S(1)}, f32[128,512]{1,0:T(8,128)S(1)}, u32[]{:S(2)}, u32[]{:S(2)}) collective-permute-start(f32[128,512]{1,0:T(8,128)S(1)} %get-tuple-element.42.own_ref), channel_id=1, source_target_pairs={{0,8},{8,0},{1,9},{9,1},{2,10},{10,2},{3,11},{11,3},{4,12},{12,4},... | collective-permute-start | bytes 786440 | tf_op jit(solution)/shard_map/ppermute | solution.py:276
  57.0 15.4 %all-to-all-start.2 = ((f32[12,16,256]{2,1,0:T(8,128)}), f32[12,16,256]{2,1,0:T(8,128)S(1)}, u32[]{:S(2)}, u32[]{:S(2)}) async-start(f32[12,16,256]{2,1,0:T(8,128)} %shard_map.107), calls=%async_computation.2 | async-start | bytes 393216 | tf_op jit(solution)/shard_map/all_to_all | solution.py:277
  61.3 55.6 %all-gather.7.cloned.1.call-start = ((), (), s32[]{:S(2)}) async-start(), calls=%async_computation.6 | async-start | bytes 1769472 | tf_op jit(solution)/shard_map/all_gather | solution.py:342
  89.7 15.6 %all-to-all-start.4 = ((f32[12,16,256]{2,1,0:T(8,128)}), f32[12,16,256]{2,1,0:T(8,128)S(1)}, u32[]{:S(2)}, u32[]{:S(2)}) async-start(f32[12,16,256]{2,1,0:T(8,128)} %shard_map.110), calls=%async_computation.4 | async-start | bytes 393216 | tf_op jit(solution)/shard_map/all_to_all | solution.py:277
  118.5 11.5 %collective-permute-start.1 = (f32[128,512]{1,0:T(8,128)S(1)}, f32[128,512]{1,0:T(8,128)S(1)}, u32[]{:S(2)}, u32[]{:S(2)}) collective-permute-start(f32[128,512]{1,0:T(8,128)S(1)} %get-tuple-element.71), channel_id=1, source_target_pairs={{0,8},{8,0},{1,9},{9,1},{2,10},{10,2},{3,11},{11,3},{4,12},{12,4},... | collective-permute-start | bytes 786440 | tf_op jit(solution)/shard_map/ppermute | solution.py:276
Sparse Core Ops, SparseCore 0:
  23.3 30.8 all-gather.4
  74.2 28.9 all-gather.6

commit v6 on v5

--- a/solution.py
+++ b/solution.py
@@ -194,10 +194,15 @@
     )
 
 
-def one_kernel(q_ref, c_ref, w_ref, zero_ref, out_ref):
+def one_kernel(q_ref, c_ref, w_ref, zero_ref, out_ref, one_ref, sems):
+    first = pltpu.make_async_copy(zero_ref, out_ref.at[0], sems.at[0])
+    first.start()
     w_gate, w_up, w_down = [split(w) for w in parts(w_ref, w_ref.shape[1] // 3)]
-    out_ref[0] = zero_ref[...]
-    out_ref[1] = query_grad(q_ref[...], c_ref[...], w_gate, w_up, w_down, NT, NN)
+    one_ref[...] = query_grad(q_ref[...], c_ref[...], w_gate, w_up, w_down, NT, NN)
+    second = pltpu.make_async_copy(one_ref, out_ref.at[1], sems.at[1])
+    second.start()
+    first.wait()
+    second.wait()
 
 
 def prepare_kernel(
@@ -375,7 +380,15 @@
         scratch_shapes=[pltpu.SemaphoreType.DMA((3,))],
     )(d_all, *loaded, *[hold(a) for a in (new_all, queries, grad_out)])
     new_all, q_one, c_one = ones
-    grad_queries = call(one_kernel, f32(2, tok, width), 30 * n_mul, 2 * n_w)(q_one, c_one, new_all, zero)
+    grad_queries = call(
+        one_kernel,
+        pltpu.HBM((2, tok, width), jnp.float32),
+        30 * n_mul,
+        2 * n_w,
+        in_specs=[here] * 4,
+        out_specs=there,
+        scratch_shapes=[vmem(tok, width), pltpu.SemaphoreType.DMA((2,))],
+    )(q_one, c_one, new_all, zero)
     theirs, grad_queries = both(swap(theirs), grad_queries)
     grad_keys, grad_values = call(
         functools.partial(join_kernel, scale), [f32(tok, width)] * 2, 0, 24 * tok * width

time: 138 us -> 138 us (level)
  no operation moved by 1% of the time
where the time goes in v6:
time: 138 us
  blocking collectives  59.5 us (43%)
  starting transfers between devices  30 us (22%)
  Pallas kernels  17.2 us (12%)
  waiting for transfers between devices  16.7 us (12%)
  between operations  14.2 us (10%)
    all_to_all x2, blocking collectives, body(): exchange = lambda x: lax.all_to_all(x.reshape(n_z, piece, width), 'z', 0, 0)  33.5 us
    ppermute x2, starting transfers between devices, body(): lax.ppermute(x, 'c', [(i, (i + 1) % NC) for i in range(NC)])  22 us
    all_to_all x2, waiting for transfers between devices, body(): exchange = lambda x: lax.all_to_all(x.reshape(n_z, piece, width), 'z', 0, 0)  16.7 us
    all_to_all x1, blocking collectives, body(): inner = lax.all_to_all(inner, 'x', 0, 0)  14.4 us
    all_gather x1, blocking collectives, body(): lax.all_gather(outer, 'x', axis=0, tiled=False)  11.6 us
    all_to_all x2, starting transfers between devices, body(): exchange = lambda x: lax.all_to_all(x.reshape(n_z, piece, width), 'z', 0, 0)  7.9 us
    pallas_call x1, Pallas kernels, body(): call(zero_kernel, f32(tok, width), 30 * n_mul, 2 * n_w, in_specs=[there]...  2.92 us
  transfers between devices with their start and end apart: 6, of which 2 were waited for; matrix products, arithmetic and copies ran while one was open for 0% of the time, Pallas kernels for 8%

profile of v6, /device:TPU:1, one launch (start us, length us, event | category | flops | bytes accessed | tf_op | source)
XLA Modules:
  0.0 137.6 jit_solution(10983016836820599509)
XLA Ops:
  7.2 0.0 all-gather.5.cloned.1.call-start
  7.2 1.0 shard_map.103
  8.2 12.4 %collective-permute-start = (f32[128,512]{1,0:T(8,128)S(1)}, f32[128,512]{1,0:T(8,128)S(1)}, u32[]{:S(2)}, u32[]{:S(2)}) collective-permute-start(f32[128,512]{1,0:T(8,128)S(1)} %get-tuple-element.42.own_ref), channel_id=1, source_target_pairs={{0,8},{8,0},{1,9},{9,1},{2,10},{10,2},{3,11},{11,3},{4,12},{12,4},... | collective-permute-start | bytes 786440 | tf_op jit(solution)/shard_map/ppermute | solution.py:281
  20.7 1.3 shard_map.104
  22.0 0.0 collective-permute-done.other_ref
  22.0 1.2 shard_map.105
  23.2 0.0 all-gather.5.cloned.1.call-update
  23.2 14.4 %all_to_all.25.in_ref = f32[4,192,256]{2,1,0:T(8,128)S(1)} all-to-all(f32[4,192,256]{2,1,0:T(8,128)S(1)} %get-tuple-element.46), channel_id=1, replica_groups=mesh['z'=12,'x'=4,'c'=2,'head'=8] {'x'}, dimensions={0} | all-to-all | bytes 1572864 | tf_op jit(solution)/shard_map/all_to_all | solution.py:323
  37.7 18.6 %all_to_all.26.in_ref = f32[12,16,256]{2,1,0:T(8,128)S(1)} all-to-all(f32[12,16,256]{2,1,0:T(8,128)S(1)} %bitcast.9), channel_id=1, replica_groups=mesh['z'=12,'x'=4,'c'=2,'head'=8] {'z'}, dimensions={0} | all-to-all | bytes 393216 | tf_op jit(solution)/shard_map/all_to_all | solution.py:282
  56.3 0.7 shard_map.107
  57.0 4.4 %all-to-all-start.2 = ((f32[12,16,256]{2,1,0:T(8,128)}), f32[12,16,256]{2,1,0:T(8,128)S(1)}, u32[]{:S(2)}, u32[]{:S(2)}) async-start(f32[12,16,256]{2,1,0:T(8,128)} %shard_map.107), calls=%async_computation.2 | async-start | bytes 393216 | tf_op jit(solution)/shard_map/all_to_all | solution.py:282
  61.3 0.0 all-gather.7.cloned.1.call-start
  61.4 0.0 all-gather.5.cloned.1.call-done.from_ref
  61.4 1.6 %shard_map.108.rows_ref = f32[1024,512]{1,0:T(8,128)S(1)} custom-call(f32[1024,512]{1,0:T(8,128)} %all-gather.5.cloned.1.call-done.from_ref), custom_call_target="tpu_custom_call" | custom-call | bytes 4194304 | tf_op jit(solution)/shard_map/pallas_call | solution.py:327
  63.0 9.4 %all-to-all-done.2 = f32[12,16,256]{2,1,0:T(8,128)S(1)} async-done(((f32[12,16,256]{2,1,0:T(8,128)}), f32[12,16,256]{2,1,0:T(8,128)S(1)}, u32[]{:S(2)}, u32[]{:S(2)}) %all-to-all-start.2) | async-done | bytes 196640 | tf_op jit(solution)/shard_map/all_to_all | solution.py:282
  72.4 1.6 %shard_map.109 = (f32[192,256]{1,0:T(8,128)S(1)}, f32[192,256]{1,0:T(8,128)}) custom-call(f32[1024,512]{1,0:T(8,128)S(1)} %shard_map.108.rows_ref, f32[192,256]{1,0:T(8,128)S(1)} %bitcast.8), custom_call_target="tpu_custom_call" | custom-call | flops 603979776 | bytes 2097152 | tf_op jit(solution)/shard_map/pallas_call | solution.py:338
  74.1 0.0 all-gather.7.cloned.1.call-update
  74.1 14.9 %all_to_all.27.in_ref = f32[12,16,256]{2,1,0:T(8,128)S(1)} all-to-all(f32[12,16,256]{2,1,0:T(8,128)S(1)} %bitcast.10), channel_id=1, replica_groups=mesh['z'=12,'x'=4,'c'=2,'head'=8] {'z'}, dimensions={0} | all-to-all | bytes 393216 | tf_op jit(solution)/shard_map/all_to_all | solution.py:282
  89.0 0.7 shard_map.110
  89.7 3.5 %all-to-all-start.4 = ((f32[12,16,256]{2,1,0:T(8,128)}), f32[12,16,256]{2,1,0:T(8,128)S(1)}, u32[]{:S(2)}, u32[]{:S(2)}) async-start(f32[12,16,256]{2,1,0:T(8,128)} %shard_map.110), calls=%async_computation.4 | async-start | bytes 393216 | tf_op jit(solution)/shard_map/all_to_all | solution.py:282
  93.2 2.9 %shard_map.111.zero_ref = f32[128,256]{1,0:T(8,128)S(1)} custom-call(f32[2,128,256]{2,1,0:T(8,128)} %q_ref.3, f32[2,128,256]{2,1,0:T(8,128)} %c_ref.3, f32[1,256,512]{2,1,0:T(8,128)} %wg_hbm_ref.1, f32[1,256,512]{2,1,0:T(8,128)} %wu_hbm_ref.1, f32[1,512,256]{2,1,0:T(8,128)} %wd_hbm_ref.1), custom_call_target="tpu_custom_call" | custom-call | flops 503316480 | bytes 1572864 | tf_op jit(solution)/shard_map/pallas_call | solution.py:350
  96.2 1.9 %shard_map.112 = (f32[256,512]{1,0:T(8,128)S(1)}, f32[4,192,256]{2,1,0:T(8,128)S(1)}, f32[256,256]{1,0:T(8,128)S(1)}, f32[256,256]{1,0:T(8,128)S(1)}, f32[256,256]{1,0:T(8,128)S(1)}) custom-call(f32[256,512]{1,0:T(8,128)} %get-tuple-element.55.pair_hbm_ref, f32[4,192,256]{2,1,0:T(8,128)} %get-tuple-element.56.w_hbm_ref), custom_call_target="tpu_custom_call" | custom-call | flops 301989888 | bytes 3145728 | tf_op jit(solution)/shard_map/pallas_call | solution.py:362
  98.1 7.2 %all-to-all-done.4 = f32[12,16,256]{2,1,0:T(8,128)S(1)} async-done(((f32[12,16,256]{2,1,0:T(8,128)}), f32[12,16,256]{2,1,0:T(8,128)S(1)}, u32[]{:S(2)}, u32[]{:S(2)}) %all-to-all-start.4) | async-done | bytes 196640 | tf_op jit(solution)/shard_map/all_to_all | solution.py:282
  105.3 11.6 %all-gather = f32[768,256]{1,0:T(8,128)S(1)} all-gather(f32[192,256]{1,0:T(8,128)S(1)} %bitcast.12), channel_id=2, replica_groups=mesh['z'=12,'x'=4,'c'=2,'head'=8] {'x'}, dimensions={0}, use_global_device_ids=true | all-gather | bytes 983040 | tf_op jit(solution)/shard_map/all_gather | solution.py:372
  116.9 0.0 all-gather.7.cloned.1.call-done
  116.9 1.6 %shard_map.113 = (f32[128,512]{1,0:T(8,128)S(1)}, f32[128,512]{1,0:T(8,128)S(1)}, f32[8,192,256]{2,1,0:T(8,128)S(1)}, f32[128,256]{1,0:T(8,128)S(1)}, f32[128,256]{1,0:T(8,128)S(1)}) custom-call(f32[4,192,256]{2,1,0:T(8,128)S(1)} %bitcast.7, f32[256,512]{1,0:T(8,128)S(1)} %get-tuple-element.65.pair_ref, f32[4,192,256]{2,1,0:T(8,128)S(1)} %get-tuple-element.66.w_ref, ...), custom_call_target="tpu_custom_call" | custom-call | flops 1207959552 | bytes 2359296 | tf_op jit(solution)/shard_map/pallas_call | solution.py:373
  118.5 9.6 %collective-permute-start.1 = (f32[128,512]{1,0:T(8,128)S(1)}, f32[128,512]{1,0:T(8,128)S(1)}, u32[]{:S(2)}, u32[]{:S(2)}) collective-permute-start(f32[128,512]{1,0:T(8,128)S(1)} %get-tuple-element.71), channel_id=1, source_target_pairs={{0,8},{8,0},{1,9},{9,1},{2,10},{10,2},{3,11},{11,3},{4,12},{12,4},... | collective-permute-start | bytes 786440 | tf_op jit(solution)/shard_map/ppermute | solution.py:281
  128.1 1.9 %shard_map.114 = f32[2,128,256]{2,1,0:T(8,128)} custom-call(f32[128,256]{1,0:T(8,128)S(1)} %get-tuple-element.72.q_ref, f32[128,256]{1,0:T(8,128)S(1)} %get-tuple-element.73.c_ref, f32[8,192,256]{2,1,0:T(8,128)S(1)} %get-tuple-element.74.w_ref, f32[128,256]{1,0:T(8,128)S(1)} %shard_map.111.zero_ref), custom_call_target="tpu_custom_call" | custom-call | flops 503316480 | bytes 1572864 | tf_op jit(solution)/shard_map/pallas_call | solution.py:383
  130.0 0.0 collective-permute-done.1.got_ref
  130.0 0.7 shard_map.115
  (1 shorter events, 0.0 us)
Async XLA Ops:
  7.2 54.2 %all-gather.5.cloned.1.call-start = ((), (), s32[]{:S(2)}) async-start(), calls=%async_computation.5 | async-start | bytes 2359296 | tf_op jit(solution)/shard_map/all_gather | solution.py:322
  8.2 13.8 %collective-permute-start = (f32[128,512]{1,0:T(8,128)S(1)}, f32[128,512]{1,0:T(8,128)S(1)}, u32[]{:S(2)}, u32[]{:S(2)}) collective-permute-start(f32[128,512]{1,0:T(8,128)S(1)} %get-tuple-element.42.own_ref), channel_id=1, source_target_pairs={{0,8},{8,0},{1,9},{9,1},{2,10},{10,2},{3,11},{11,3},{4,12},{12,4},... | collective-permute-start | bytes 786440 | tf_op jit(solution)/shard_map/ppermute | solution.py:281
  57.0 15.4 %all-to-all-start.2 = ((f32[12,16,256]{2,1,0:T(8,128)}), f32[12,16,256]{2,1,0:T(8,128)S(1)}, u32[]{:S(2)}, u32[]{:S(2)}) async-start(f32[12,16,256]{2,1,0:T(8,128)} %shard_map.107), calls=%async_computation.2 | async-start | bytes 393216 | tf_op jit(solution)/shard_map/all_to_all | solution.py:282
  61.3 55.6 %all-gather.7.cloned.1.call-start = ((), (), s32[]{:S(2)}) async-start(), calls=%async_computation.6 | async-start | bytes 1769472 | tf_op jit(solution)/shard_map/all_gather | solution.py:347
  89.7 15.6 %all-to-all-start.4 = ((f32[12,16,256]{2,1,0:T(8,128)}), f32[12,16,256]{2,1,0:T(8,128)S(1)}, u32[]{:S(2)}, u32[]{:S(2)}) async-start(f32[12,16,256]{2,1,0:T(8,128)} %shard_map.110), calls=%async_computation.4 | async-start | bytes 393216 | tf_op jit(solution)/shard_map/all_to_all | solution.py:282
  118.5 11.5 %collective-permute-start.1 = (f32[128,512]{1,0:T(8,128)S(1)}, f32[128,512]{1,0:T(8,128)S(1)}, u32[]{:S(2)}, u32[]{:S(2)}) collective-permute-start(f32[128,512]{1,0:T(8,128)S(1)} %get-tuple-element.71), channel_id=1, source_target_pairs={{0,8},{8,0},{1,9},{9,1},{2,10},{10,2},{3,11},{11,3},{4,12},{12,4},... | collective-permute-start | bytes 786440 | tf_op jit(solution)/shard_map/ppermute | solution.py:281
Sparse Core Ops, SparseCore 0:
  23.3 30.8 all-gather.4
  74.2 28.9 all-gather.6
